TPU v7x, 128 devices: a whole 4x4x4 slice. The times are simulated.
128 devices in a mesh: ctx: 16 (over x, z), head: 8 (over y, core).
Axes of the slice: x: 4, y: 4, z: 4, core: 2. Of those that a mesh axis runs over, the one named last changes fastest.
Arguments:
- queries: bfloat16 [8192, 8192], P('ctx', 'head'), may hold values from -6 to 6
- key_rows: bfloat16 [8192, 8192], P('ctx', 'head'), may hold values from -8 to 8
- value_rows: bfloat16 [8192, 8192], P('ctx', 'head'), may hold values from -6 to 6
- log_decay: float32 [8192, 64], P('ctx', 'head'), may hold values from -3 to 0, as said below
- write_rate: float32 [8192, 64], P('ctx', 'head'), may hold values from 0 to 1, as said below
- level_weights: float32 [8192, 320], P('ctx', 'head'), may hold values from 0.25 to 2.5
- block_levels: int32 [128], P('ctx'), may hold values from 1 to 5
Outputs:
- mixed: bfloat16 [8192, 8192], P(('ctx', 'head'))
Inputs may be any that keep to these rules, and one draw needn't show every extreme that they name: `log_decay`: strictly negative. `write_rate`: strictly positive.
All inputs are finite; a program needn't handle non-finite values.
Results may differ from a plain program's by a relative error of at most 0.0087.
Values may be sent and summed in bfloat16 or wider, within the bound.
A program may use at most 128 MiB of HBM per device.

v0:
```python
import jax
import jax.numpy as jnp
from jax import lax
from jax.sharding import PartitionSpec as P

BLOCK = 64
LEVELS = 5


precise = lax.Precision.HIGHEST


def partner(array, axis, bit):
    return lax.ppermute(array, axis, [(i, i ^ 1 << bit) for i in range(lax.axis_size(axis))])


def matmul_hi(left_mat, right_mat):
    return jnp.matmul(left_mat, right_mat, precision=precise)


def low_product(form, left_op, right_op):
    return jnp.einsum(form, left_op, right_op, preferred_element_type=jnp.float32)


def to_blocks(tensor):
    block_count = tensor.shape[0] // BLOCK
    shaped = tensor.reshape((block_count, BLOCK) + tensor.shape[1:])
    return jnp.moveaxis(shaped, 2, 0)


def prepare(query_in, key_in, value_in, head_count):
    length = query_in.shape[0]
    query_low = query_in.reshape(length, head_count, -1)
    key_f = key_in.astype(jnp.float32).reshape(length, head_count, -1)
    key_low = (key_f * lax.rsqrt(jnp.sum(key_f * key_f, axis=-1, keepdims=True) + 1e-06)).astype(
        jnp.bfloat16
    )
    value_f = value_in.astype(jnp.float32).reshape(length, head_count, -1)
    return (query_low, key_low, value_f)


def local_pass(query_low, key_low, value_f, log_decay, write_rate):
    head_count = key_low.shape[1]
    head_width = key_low.shape[2]
    query_b = to_blocks(query_low)
    key_lb = to_blocks(key_low)
    key_b = key_lb.astype(jnp.float32)
    value_b = to_blocks(value_f)
    cum_log = jnp.cumsum(to_blocks(log_decay), axis=-1)
    rate_b = to_blocks(write_rate)
    places = jnp.arange(BLOCK)
    lower_tri = places[:, None] >= places[None, :]
    strict_tri = places[:, None] > places[None, :]
    log_gaps = cum_log[..., :, None] - cum_log[..., None, :]
    decay_incl = jnp.exp(jnp.where(lower_tri, log_gaps, -1e30))
    decay_strict = jnp.where(strict_tri, decay_incl, 0.0)
    gram_keys = jnp.einsum("hbik,hbjk->hbij", key_b, key_b, precision=precise)
    strict_part = rate_b[..., :, None] * decay_strict * gram_keys
    right_side = jnp.concatenate(
        [rate_b[..., None] * value_b, (rate_b * jnp.exp(cum_log))[..., None] * key_b], axis=-1
    )
    solved = jax.scipy.linalg.solve_triangular(
        strict_part, right_side, lower=True, unit_diagonal=True
    )
    wy_values = solved[..., :head_width]
    wy_keys = solved[..., head_width:]
    inputs = jnp.concatenate([wy_values, jnp.zeros_like(wy_keys)], axis=-1)
    key_tail = jnp.exp(cum_log[..., -1:] - cum_log)[..., None] * key_b
    block_fall = jnp.exp(cum_log[..., -1])
    scores_low = (low_product("hbik,hbjk->hbij", query_b, key_lb) * decay_incl).astype(jnp.bfloat16)
    initial = jnp.concatenate(
        [
            jnp.zeros((head_count, head_width, head_width), key_b.dtype),
            jnp.broadcast_to(
                jnp.eye(head_width, dtype=key_b.dtype), (head_count, head_width, head_width)
            ),
        ],
        axis=-1,
    )

    def advance(carry_state, slices):
        wy_part, given_vals, tail_keys, fall_now = slices
        errors = given_vals - jnp.einsum("hcd,hde->hce", wy_part, carry_state, precision=precise)
        updated = fall_now[:, None, None] * carry_state + jnp.einsum(
            "hcd,hce->hde", tail_keys, errors, precision=precise
        )
        return (updated, (carry_state, errors))

    end_state, (starts, errors) = lax.scan(
        advance,
        initial,
        (
            jnp.moveaxis(wy_keys, 1, 0),
            jnp.moveaxis(inputs, 1, 0),
            jnp.moveaxis(key_tail, 1, 0),
            jnp.moveaxis(block_fall, 1, 0),
        ),
    )
    mixed = jnp.exp(cum_log)[..., None] * low_product(
        "hbcd,bhde->hbce", query_b, starts.astype(jnp.bfloat16)
    )
    mixed = mixed + low_product("hbij,bhje->hbie", scores_low, errors.astype(jnp.bfloat16))
    mixed = jnp.moveaxis(mixed, 0, 2).reshape(-1, head_count, 2 * head_width)
    return (mixed, end_state)


def join_runs(left_run, right_run):
    head_width = left_run.shape[-2]
    return matmul_hi(right_run[..., head_width:], left_run) + jnp.concatenate(
        [right_run[..., :head_width], jnp.zeros_like(right_run[..., :head_width])], axis=-1
    )


def finish(mixed, carried, weights, levels_in):
    length, head_count, twice = mixed.shape
    head_width = twice // 2
    near_part = mixed[..., :head_width]
    row_part = mixed[..., head_width:].astype(jnp.bfloat16)
    far_part = low_product("thd,lhde->thle", row_part, carried.astype(jnp.bfloat16))
    terms = jnp.concatenate([near_part[:, :, None], far_part], axis=2)
    level_ids = jnp.arange(LEVELS)
    keep_mask = (level_ids[None, :] < levels_in[:, None]).astype(weights.dtype)
    scaled = (
        weights.reshape(length // BLOCK, BLOCK, head_count, LEVELS) * keep_mask[:, None, None, :]
    )
    scaled = scaled.reshape(length, head_count, LEVELS)
    total = jnp.sum(scaled[..., None] * terms, axis=2)
    return total.astype(jnp.bfloat16).reshape(length, head_count * head_width)


def per_device(queries, key_rows, value_rows, log_decay, write_rate, level_weights, block_levels):
    head_count = log_decay.shape[1]
    query_low, key_low, value_f = prepare(queries, key_rows, value_rows, head_count)
    mixed, own_run = local_pass(query_low, key_low, value_f, log_decay, write_rate)
    head_width = key_low.shape[2]
    bits_total = lax.axis_size("ctx").bit_length() - 1
    position = lax.axis_index("ctx")
    prefix = jnp.broadcast_to(
        jnp.eye(head_width, dtype=own_run.dtype), (head_count, head_width, head_width)
    )
    carried = []
    for section in range(bits_total):
        upper = position >> section & 1 == 1
        other_run = partner(own_run, "ctx", section)
        carried.append(jnp.where(upper, matmul_hi(prefix, other_run[..., :head_width]), 0.0))
        prefix = jnp.where(upper, matmul_hi(prefix, other_run[..., head_width:]), prefix)
        if section + 1 < bits_total:
            left_run = jnp.where(upper, other_run, own_run)
            right_run = jnp.where(upper, own_run, other_run)
            own_run = join_runs(left_run, right_run)
    stacked = jnp.stack(carried, axis=0)
    outputs = finish(mixed, stacked, level_weights, block_levels)
    return lax.all_to_all(outputs, "head", split_axis=0, concat_axis=1, tiled=True)


def solution(mesh):
    in_specs = (
        P("ctx", "head"),
        P("ctx", "head"),
        P("ctx", "head"),
        P("ctx", "head"),
        P("ctx", "head"),
        P("ctx", "head"),
        P("ctx"),
    )
    out_specs = P(("ctx", "head"), None)
    return jax.shard_map(
        per_device, mesh=mesh, in_specs=in_specs, out_specs=out_specs, check_vma=False
    )
```

profile of v0, /device:TPU:1, one launch (start us, length us, event | category | flops | bytes accessed | tf_op | source)
XLA Modules:
  0.0 529.3 jit_solution(8224274965342514809)
XLA Ops:
  0.0 2.9 fusion.14
  2.9 1.6 convert_bitcast_fusion
  4.7 1.7 reduce_window_sum.13
  6.6 2.1 copy.71
  9.5 2.2 copy.70
  12.5 3.0 convert_multiply_fusion.1
  15.5 2.2 add_bitcast_fusion
  17.7 316.0 %custom-call.4 = f32[8,8,1,64,64]{3,4,2,1,0:T(8,128)} custom-call(f32[8,8,1,64,64]{4,3,2,1,0:T(8,128)} %add_bitcast_fusion), custom_call_target="InvertDiagBlocksLowerTriangular" | custom-call | tf_op jit(solution)/shard_map/jit(_solve_triangular)/vmap(vmap())/triangular_solve | solution.py:62
  333.7 6.0 %fusion.8 = f32[8,8,64,256]{3,2,1,0:T(8,128)S(1)} fusion(f32[8,8,64,128]{3,2,1,0:T(8,128)S(1)} %get-tuple-element.100, f32[8,8,64,128]{3,2,1,0:T(8,128)} %get-tuple-element.110, f32[8,8,1,64,64]{3,4,2,1,0:T(8,128)} %custom-call.4), kind=kOutput, calls=%fused_computation.14 | convolution fusion | flops 806354944 | bytes 9437184 | tf_op jit(solution)/shard_map/jit(_solve_triangular)/vmap(vmap())/triangular_solve | solution.py:62
  339.7 1.5 slice_bitcast_fusion.1
  341.3 2.5 select_bitcast_fusion
  343.8 2.0 bitcast_multiply_fusion.3
  346.0 1.6 broadcast_in_dim.65
  347.6 45.7 %while.14 = (s32[]{:T(128)}, f32[8,128,256]{2,1,0:T(8,128)S(1)}, bf16[8,8,128,256]{3,2,1,0:T(8,128)(2,1)}, bf16[8,8,64,256]{3,2,1,0:T(8,128)(2,1)}, f32[8,8]{1,0...) while((s32[]{:T(128)}, f32[8,128,256]{2,1,0:T(8,128)S(1)}, ...), condition=%wide.region_3.4_spmd, body=%wide.region_2.3_spmd.sunk | while | flops 403308544 | bytes 7866561 | solution.py:89
  347.6 2.6 bitcast_dynamic-update-slice_fusion.4
  350.1 0.9 bitcast_dynamic-update-slice_fusion.5
  351.0 2.3 convolution_add_fusion.5
  353.3 2.6 bitcast_dynamic-update-slice_fusion.4
  355.9 0.9 bitcast_dynamic-update-slice_fusion.5
  356.7 2.3 convolution_add_fusion.5
  359.0 2.6 bitcast_dynamic-update-slice_fusion.4
  361.6 0.9 bitcast_dynamic-update-slice_fusion.5
  362.5 2.3 convolution_add_fusion.5
  364.7 2.6 bitcast_dynamic-update-slice_fusion.4
  367.3 0.8 bitcast_dynamic-update-slice_fusion.5
  368.2 2.3 convolution_add_fusion.5
  370.4 2.6 bitcast_dynamic-update-slice_fusion.4
  373.0 0.9 bitcast_dynamic-update-slice_fusion.5
  373.9 2.3 convolution_add_fusion.5
  376.1 2.6 bitcast_dynamic-update-slice_fusion.4
  378.7 0.9 bitcast_dynamic-update-slice_fusion.5
  379.6 2.3 convolution_add_fusion.5
  381.9 2.5 bitcast_dynamic-update-slice_fusion.4
  384.4 0.8 bitcast_dynamic-update-slice_fusion.5
  385.3 2.3 convolution_add_fusion.5
  387.5 2.5 bitcast_dynamic-update-slice_fusion.4
  390.1 0.9 bitcast_dynamic-update-slice_fusion.5
  391.0 2.3 convolution_add_fusion.5
  393.3 2.7 collective-permute-start
  396.0 22.9 %collective-permute-done = f32[8,128,256]{2,1,0:T(8,128)S(1)} collective-permute-done((f32[8,128,256]{2,1,0:T(8,128)S(1)}, f32[8,128,256]{2,1,0:T(8,128)S(1)}, u32[]{:S(2)}, u32[]{:S(2)}) %collective-permute-start) | collective-permute-done | bytes 1048608 | tf_op jit(solution)/shard_map/ppermute | solution.py:14
  419.0 2.1 convolution_add_fusion.3
  421.0 3.2 collective-permute-start.1
  424.2 1.5 copy.69
  425.7 5.2 fusion.12
  430.9 15.5 %collective-permute-done.1 = f32[8,128,256]{2,1,0:T(8,128)S(1)} collective-permute-done((f32[8,128,256]{2,1,0:T(8,128)}, f32[8,128,256]{2,1,0:T(8,128)S(1)}, u32[]{:S(2)}, u32[]{:S(2)}) %collective-permute-start.1) | collective-permute-done | bytes 1048608 | tf_op jit(solution)/shard_map/ppermute | solution.py:14
  446.6 3.4 convolution_add_fusion.2
  450.0 1.2 collective-permute-start.2
  451.2 6.3 %bitcast_add_fusion = f32[8,64,8,256]{3,1,0,2:T(8,128)} fusion(f32[8,8,256,64]{2,3,1,0:T(8,128)} %fusion.12, bf16[8,8,64,256]{3,2,1,0:T(8,128)(2,1)} %get-tuple-element.50, f32[8,64,8]{1,0,2:T(8,128)S(1)} %get-tuple-element.104, bf16[8,64,8,128]{3,1,0,2:T(8,128)(2,1)S(1)} %get-tuple-element.101, f32[8,8,64]{2,1,0:T(8,128)S(1)} %reduce_window_sum.13, ...), kind=kOutput, calls=%fused_computation.18 | convolution fusion | flops 204472320 | bytes 12619776 | tf_op jit(solution)/shard_map/hbij,bhje->hbie/dot_general | solution.py:22
  457.5 3.1 slice_bitcast_fusion
  460.6 3.0 copy.57
  464.4 8.5 %collective-permute-done.2 = f32[8,128,256]{2,1,0:T(8,128)} collective-permute-done((f32[8,128,256]{2,1,0:T(8,128)}, f32[8,128,256]{2,1,0:T(8,128)}, u32[]{:S(2)}, u32[]{:S(2)}) %collective-permute-start.2) | collective-permute-done | bytes 1048608 | tf_op jit(solution)/shard_map/ppermute | solution.py:14
  472.9 1.4 broadcast_select_fusion
  474.3 2.3 convolution_add_fusion.1
  476.6 3.0 collective-permute-start.3
  480.2 0.6 fusion.25
  480.9 0.6 convolution_select_fusion.1
  481.6 1.8 fusion.24
  483.4 1.7 convolution_select_fusion
  485.1 15.1 %collective-permute-done.3 = f32[8,128,256]{2,1,0:T(8,128)S(1)} collective-permute-done((f32[8,128,256]{2,1,0:T(8,128)S(1)}, f32[8,128,256]{2,1,0:T(8,128)S(1)}, u32[]{:S(2)}, u32[]{:S(2)}) %collective-permute-start.3) | collective-permute-done | bytes 1048608 | tf_op jit(solution)/shard_map/ppermute | solution.py:14
  500.8 1.3 convolution_bitcast_fusion
  502.4 1.6 fusion.7
  504.0 0.8 copy.58
  505.3 23.0 %all_to_all.16 = bf16[8,64,1024]{2,1,0:T(8,128)(2,1)S(1)} all-to-all(bf16[8,64,1024]{2,1,0:T(8,128)(2,1)S(1)} %convert_element_type.64), channel_id=1, replica_groups=mesh['ctx'=16,'head'=8] {'head'}, dimensions={0} | all-to-all | bytes 2097152 | tf_op jit(solution)/shard_map/all_to_all | solution.py:153
  528.2 1.1 copy.68
  (58 shorter events, 5.3 us)
Async XLA Ops:
  0.0 2.9 copy-start.3
  2.9 1.6 copy-start.6
  2.9 1.7 copy-start.7
  9.5 2.2 copy-start.4
  339.7 1.5 copy-start.8
  393.3 25.6 %collective-permute-start = (f32[8,128,256]{2,1,0:T(8,128)S(1)}, f32[8,128,256]{2,1,0:T(8,128)S(1)}, u32[]{:S(2)}, u32[]{:S(2)}) collective-permute-start(f32[8,128,256]{2,1,0:T(8,128)S(1)} %get-tuple-element.51), channel_id=1, source_target_pairs={{0,8},{8,0},{16,24},{24,16},{32,40},{40,32},{48,56},{56,48},{64,72... | collective-permute-start | bytes 3145736 | tf_op jit(solution)/shard_map/ppermute | solution.py:14
  421.0 25.4 %collective-permute-start.1 = (f32[8,128,256]{2,1,0:T(8,128)}, f32[8,128,256]{2,1,0:T(8,128)S(1)}, u32[]{:S(2)}, u32[]{:S(2)}) collective-permute-start(f32[8,128,256]{2,1,0:T(8,128)} %convolution_add_fusion.3), channel_id=1, source_target_pairs={{0,16},{8,24},{16,0},{24,8},{32,48},{40,56},{48,32},{56,40},{64,80... | collective-permute-start | bytes 3145736 | tf_op jit(solution)/shard_map/ppermute | solution.py:14
  425.7 5.2 copy-start.1
  450.0 22.9 %collective-permute-start.2 = (f32[8,128,256]{2,1,0:T(8,128)}, f32[8,128,256]{2,1,0:T(8,128)}, u32[]{:S(2)}, u32[]{:S(2)}) collective-permute-start(f32[8,128,256]{2,1,0:T(8,128)} %convolution_add_fusion.2), channel_id=1, source_target_pairs={{0,32},{8,40},{16,48},{24,56},{32,0},{40,8},{48,16},{56,24},{64,96... | collective-permute-start | bytes 3145736 | tf_op jit(solution)/shard_map/ppermute | solution.py:14
  460.6 3.0 copy-start.5
  460.6 3.0 copy-start.9
  476.6 23.6 %collective-permute-start.3 = (f32[8,128,256]{2,1,0:T(8,128)S(1)}, f32[8,128,256]{2,1,0:T(8,128)S(1)}, u32[]{:S(2)}, u32[]{:S(2)}) collective-permute-start(f32[8,128,256]{2,1,0:T(8,128)S(1)} %convolution_add_fusion.1), channel_id=1, source_target_pairs={{0,64},{8,72},{16,80},{24,88},{32,96},{40,104},{48,112},{56,120},{... | collective-permute-start | bytes 3145736 | tf_op jit(solution)/shard_map/ppermute | solution.py:14
  481.5 19.3 %copy-start = (f32[8,64,8,256]{3,1,0,2:T(8,128)S(1)}, f32[8,64,8,256]{3,1,0,2:T(8,128)}, u32[]{:S(2)}) copy-start(f32[8,64,8,256]{3,1,0,2:T(8,128)} %bitcast_add_fusion) | copy-start | bytes 12582916
  500.8 1.6 copy-start.2
where the time goes:
time: 530 us; the launch traced here: 529 us
  other arithmetic  334 us (63%)
  matrix products  74.1 us (14%)
  waiting for transfers between devices  61.9 us (12%)
  local copies, waits for them, and re-layouts  25.7 us (5%)
  blocking collectives  23 us (4%)
  starting transfers between devices  10.1 us (2%)
    another operation x3, other arithmetic, local_pass(): jax.scipy.linalg.solve_triangular(strict_part, right_side, lower=True, un...  316 us
    ppermute x4, waiting for transfers between devices, partner(): lax.ppermute(array, axis, [(i, i ^ 1 << bit) for i in range(lax.axis_size...  61.9 us
    all_to_all x1, blocking collectives, per_device(): lax.all_to_all(outputs, 'head', split_axis=0, concat_axis=1, tiled=True)  23 us
    dot_general x8, matrix products, advance(): jnp.einsum('hcd,hde->hce', wy_part, carry_state, precision=precise)  20.5 us
    dot_general x8, matrix products, advance(): jnp.einsum('hcd,hce->hde', tail_keys, errors, precision=precise)  18.1 us
    dot_general x10, matrix products, matmul_hi(): return jnp.matmul(left_mat, right_mat, precision=precise)  14.4 us
    dot_general x3, matrix products, low_product(): jnp.einsum(form, left_op, right_op, preferred_element_type=jnp.float32)  12.8 us
  transfers between devices with their start and end apart: 4, of which 4 were waited for; matrix products, arithmetic and copies ran while one was open for 5% of the time, Pallas kernels for 0%

commit v1 on v0

v1 whole, which is shorter than its diff:
```python
import jax
import jax.numpy as jnp
from jax import lax
from jax.experimental import pallas as pl
from jax.experimental.pallas import tpu as pltpu
from jax.sharding import PartitionSpec as P

BLOCK = 64
LEVELS = 5
F32, BF = jnp.float32, jnp.bfloat16
C = 128
NCH = 4
HP = 2
NT = ((1,), (1,))
TN = ((0,), (0,))


def dotf(a, b, dims=((1,), (0,))):
    return lax.dot_general(a, b, (dims, ((), ())), preferred_element_type=F32)


def split(x):
    high = x.astype(BF)
    return high, (x - high.astype(F32)).astype(BF)


def dot2(a, b, dims=((1,), (0,))):
    high, low = split(a)
    return dotf(high, b, dims) + dotf(low, b, dims)


def inverses(lowers, ii, jj):
    diff = lax.bitwise_xor(ii, jj)
    eye = (ii == jj).astype(F32)
    low_b = [m.astype(BF) for m in lowers]
    zero = jnp.zeros((), BF)
    inv = [eye - jnp.where(diff == 1, m, 0.0) for m in lowers]
    for b in (2, 4, 8):
        mask = (diff >= b) & (diff < 2 * b)
        cross = [jnp.where(mask, m, zero) for m in low_b]
        inv_b = [x.astype(BF) for x in inv]
        ys = [dotf(c, x).astype(BF) for c, x in zip(cross, inv_b)]
        zs = [dotf(x, y) for x, y in zip(inv_b, ys)]
        inv = [x - z for x, z in zip(inv, zs)]
    for b in (16, 32, 64):
        mask = (diff >= b) & (diff < 2 * b)

        def lower_rows(a):
            return jnp.concatenate([a[o + b : o + 2 * b] for o in range(0, C, 2 * b)], 0)

        mask_low = lower_rows(mask)
        cross = [jnp.where(mask_low, lower_rows(m), zero) for m in low_b]
        inv_b = [x.astype(BF) for x in inv]
        ys = [dotf(c, x).astype(BF) for c, x in zip(cross, inv_b)]
        pad = jnp.zeros((b, C), BF)
        full = []
        for y in ys:
            parts = []
            for k in range(C // (2 * b)):
                parts += [pad, y[k * b : (k + 1) * b]]
            full.append(jnp.concatenate(parts, 0))
        zs = [dotf(lower_rows(x), y) for x, y in zip(inv_b, full)]
        out = []
        for x, z in zip(inv, zs):
            parts = []
            for k in range(C // (2 * b)):
                o = k * 2 * b
                parts += [x[o : o + b], x[o + b : o + 2 * b] - z[k * b : (k + 1) * b]]
            out.append(jnp.concatenate(parts, 0))
        inv = out
    inv_b = [x.astype(BF) for x in inv]
    prods = [dot2(m, x) for m, x in zip(lowers, inv_b)]
    errs = [(eye - x.astype(F32) - p).astype(BF) for x, p in zip(inv_b, prods)]
    return [x.astype(F32) + dotf(x, e) for x, e in zip(inv_b, errs)]


def setup_gates(decay, rate, g_ref, gt_ref, bt_ref):
    ii = lax.broadcasted_iota(jnp.int32, (C, C), 0)
    jj = lax.broadcasted_iota(jnp.int32, (C, C), 1)
    tri = (ii >= jj).astype(F32)
    for c in range(NCH):
        sl = slice(c * C, (c + 1) * C)
        g_ref[sl, :] = jnp.dot(tri, decay[sl, :], precision=lax.Precision.HIGHEST, preferred_element_type=F32)
    gt_ref[...] = g_ref[...].T
    bt_ref[...] = rate.T


def local_heads(heads, q, k, v, g_all, b_all, gt_ref, bt_ref):
    ii = lax.broadcasted_iota(jnp.int32, (C, C), 0)
    jj = lax.broadcasted_iota(jnp.int32, (C, C), 1)
    tri = ii >= jj
    strict = ii > jj
    eye = (ii == jj).astype(F32)
    lane = lax.broadcasted_iota(jnp.int32, g_all.shape, 1)
    kns, qs, vs, gcs, grs, brs, bcs = [], [], [], [], [], [], []
    for n, h in enumerate(heads):
        kf = k[n].astype(F32)
        kn = (kf * lax.rsqrt(jnp.sum(kf * kf, axis=-1, keepdims=True) + 1e-6)).astype(BF)
        gcol = jnp.sum(jnp.where(lane == h, g_all, 0.0), axis=1, keepdims=True)
        bcol = jnp.sum(jnp.where(lane == h, b_all, 0.0), axis=1, keepdims=True)
        grow = gt_ref[pl.ds(h, 1), :]
        brow = bt_ref[pl.ds(h, 1), :]
        for c in range(NCH):
            sl = slice(c * C, (c + 1) * C)
            kns.append(kn[sl])
            qs.append(q[n][sl])
            vs.append(v[n][sl])
            gcs.append(gcol[sl])
            bcs.append(bcol[sl])
            grs.append(grow[:, sl])
            brs.append(brow[:, sl])
    falls = [jnp.exp(jnp.where(tri, gc - gr, -1e30)) for gc, gr in zip(gcs, grs)]
    gram = [dotf(a, a, NT) for a in kns]
    qk = [dotf(a, b, NT) for a, b in zip(qs, kns)]
    lowers = [jnp.where(strict, bc * d * g, 0.0) for bc, d, g in zip(bcs, falls, gram)]
    scores = [(a * d).astype(BF) for a, d in zip(qk, falls)]
    inv = inverses(lowers, ii, jj)
    egr = [jnp.exp(g) for g in grs]
    egc = [jnp.exp(g) for g in gcs]
    wv = [dot2(x * b, vv) for x, b, vv in zip(inv, brs, vs)]
    wk = [dot2(x * (b * e), kk) for x, b, e, kk in zip(inv, brs, egr, kns)]
    count = len(heads)
    near, rows = [[] for _ in heads], [[] for _ in heads]
    pair = [None] * count
    for c in range(NCH):
        for n in range(count):
            i = n * NCH + c
            glast = gcs[i][C - 1 : C, :]
            fall = jnp.exp(glast)
            tail = jnp.exp(glast - gcs[i])
            if c == 0:
                errors = jnp.concatenate([wv[i], -wk[i]], axis=1)
            else:
                pair_b = pair[n].astype(BF)
                errors = jnp.concatenate([wv[i], jnp.zeros_like(wv[i])], axis=1) - dotf(wk[i].astype(BF), pair_b)
            mixed = dotf(scores[i], errors.astype(BF))
            if c == 0:
                near_c = mixed[:, :128]
                rows_c = egc[i] * qs[i].astype(F32) + mixed[:, 128:]
            else:
                mixed = mixed + egc[i] * dotf(qs[i], pair_b)
                near_c = mixed[:, :128]
                rows_c = mixed[:, 128:]
            near[n].append(near_c)
            rows[n].append(rows_c.astype(BF))
            high, low = split(tail * errors)
            grown = dotf(kns[i], high, TN) + dotf(kns[i], low, TN)
            if c == 0:
                pair[n] = jnp.concatenate([jnp.zeros((128, 128), F32), fall * eye], axis=1) + grown
            else:
                pair[n] = fall * pair[n] + grown
    near = [jnp.concatenate(x, 0) for x in near]
    rows = [jnp.concatenate(x, 0) for x in rows]
    return near, rows, pair


def local_kernel(q_ref, k_ref, v_ref, ld_ref, b_ref, near_ref, rows_ref, run_ref, g_ref, gt_ref, bt_ref):
    p = pl.program_id(0)

    @pl.when(p == 0)
    def _():
        setup_gates(ld_ref[...], b_ref[...], g_ref, gt_ref, bt_ref)

    heads = [p * HP + n for n in range(HP)]

    def cut(ref):
        return [ref[:, n * 128 : (n + 1) * 128] for n in range(HP)]

    near, rows, pair = local_heads(
        heads, cut(q_ref), cut(k_ref), cut(v_ref), g_ref[...], b_ref[...], gt_ref, bt_ref
    )
    for n in range(HP):
        near_ref[:, n * 128 : (n + 1) * 128] = near[n]
        rows_ref[:, n * 128 : (n + 1) * 128] = rows[n]
        run_ref[n] = pair[n]


def local_call(q, k, v, decay, rate):
    wide = pl.BlockSpec((512, HP * 128), lambda p: (0, p))
    gate = pl.BlockSpec((512, 8), lambda p: (0, 0))
    run = pl.BlockSpec((HP, 128, 256), lambda p: (p, 0, 0))
    return pl.pallas_call(
        local_kernel,
        grid=(8 // HP,),
        in_specs=[wide, wide, wide, gate, gate],
        out_specs=[wide, wide, run],
        out_shape=[
            jax.ShapeDtypeStruct((512, 1024), F32),
            jax.ShapeDtypeStruct((512, 1024), BF),
            jax.ShapeDtypeStruct((8, 128, 256), F32),
        ],
        scratch_shapes=[pltpu.VMEM((512, 8), F32), pltpu.VMEM((8, 512), F32), pltpu.VMEM((8, 512), F32)],
        compiler_params=pltpu.CompilerParams(vmem_limit_bytes=56 << 20),
        name="local_pass",
    )(q, k, v, decay, rate)


def partner(array, axis, bit):
    return lax.ppermute(array, axis, [(i, i ^ 1 << bit) for i in range(lax.axis_size(axis))])


def low_product(form, left_op, right_op):
    return jnp.einsum(form, left_op, right_op, preferred_element_type=F32)


def finish(near, rows, carried, weights, levels_in):
    length, wide = near.shape
    head_count = wide // 128
    near_part = near.reshape(length, head_count, 128)
    row_part = rows.reshape(length, head_count, 128)
    far_part = low_product("thd,lhde->thle", row_part, carried.astype(BF))
    terms = jnp.concatenate([near_part[:, :, None], far_part], axis=2)
    level_ids = jnp.arange(LEVELS)
    keep_mask = (level_ids[None, :] < levels_in[:, None]).astype(weights.dtype)
    scaled = weights.reshape(length // BLOCK, BLOCK, head_count, LEVELS) * keep_mask[:, None, None, :]
    scaled = scaled.reshape(length, head_count, LEVELS)
    total = jnp.sum(scaled[..., None] * terms, axis=2)
    return total.astype(BF).reshape(length, wide)


def per_device(queries, key_rows, value_rows, log_decay, write_rate, level_weights, block_levels):
    near, rows, own = local_call(queries, key_rows, value_rows, log_decay, write_rate)
    bits_total = lax.axis_size("ctx").bit_length() - 1
    position = lax.axis_index("ctx")
    prefix = jnp.broadcast_to(jnp.eye(128, dtype=F32), (8, 128, 128))
    carried = []
    for section in range(bits_total):
        upper = position >> section & 1 == 1
        own_b = own.astype(BF)
        other_b = partner(own_b, "ctx", section)
        left = jnp.where(upper, other_b, own_b)
        both = jnp.matmul(prefix.astype(BF), other_b, preferred_element_type=F32)
        carried.append(jnp.where(upper, both[..., :128], 0.0))
        prefix = jnp.where(upper, both[..., 128:], prefix)
        if section + 1 < bits_total:
            right_trans = jnp.where(upper, own_b, other_b)[..., 128:]
            right_state = jnp.where(upper, own, other_b.astype(F32))[..., :128]
            joined = jnp.matmul(right_trans, left, preferred_element_type=F32)
            own = joined + jnp.concatenate([right_state, jnp.zeros_like(right_state)], axis=-1)
    outputs = finish(near, rows, jnp.stack(carried, axis=0), level_weights, block_levels)
    return lax.all_to_all(outputs, "head", split_axis=0, concat_axis=1, tiled=True)


def solution(mesh):
    in_specs = (P("ctx", "head"),) * 6 + (P("ctx"),)
    out_specs = P(("ctx", "head"), None)
    return jax.shard_map(per_device, mesh=mesh, in_specs=in_specs, out_specs=out_specs, check_vma=False)
```

time: 530 us -> 110 us (0.21)
  other arithmetic: 334 us -> 3.08 us
  matrix products: 74.1 us -> 8.67 us
  waiting for transfers between devices: 61.9 us -> 35.6 us
  Pallas kernels: 0 us -> 20.7 us
  local copies, waits for them, and re-layouts: 25.7 us -> 9.06 us
    another operation x4 -> x3, other arithmetic: 318 us -> 0.16 us  [per_device(): jnp.stack(carried, axis=0)]
    dot_general x30 -> x8, matrix products: 68.1 us -> 8.67 us  [the longest x3 4.22 us: per_device(): joined = jnp.matmul(right_trans, left, preferred_element_type=F32)]
    ppermute x4, waiting for transfers between devices: 61.9 us -> 35.6 us  [partner(): lax.ppermute(array, axis, [(i, i ^ 1 << bit) for i in range(lax.axis_size...]
    pallas_call x0 -> x1, Pallas kernels: none -> 20.7 us  [local_call(): pl.pallas_call(local_kernel, grid=(8 // HP,), in_specs=[wide, wide, wide,...]
    broadcast_in_dim x4 -> x0, local copies, waits for them, and re-layouts: 7.66 us -> none  [the longest x2 6.05 us: finish(): terms = jnp.concatenate([near_part[:, :, None], far_part], axis=2)]
    dynamic_update_slice x8 -> x0, local copies, waits for them, and re-layouts: 6.93 us -> none  [local_pass(): lax.scan(advance, initial, (jnp.moveaxis(wy_keys, 1, 0), jnp.moveaxis(inp...]
    another operation x1 -> x0, matrix products: 5.99 us -> none  [local_pass(): jax.scipy.linalg.solve_triangular(strict_part, right_side, lower=True, un...]
  transfers between devices with their start and end apart: 4 -> 4, of which waited for: 4 -> 4; matrix products, arithmetic and copies ran while one was open for 5% -> 6% of each run, Pallas kernels for 0% -> 0%
where the time goes in v1:
time: 110 us
  waiting for transfers between devices  35.6 us (32%)
  blocking collectives  22.9 us (21%)
  Pallas kernels  20.7 us (19%)
  starting transfers between devices  9.84 us (9%)
  local copies, waits for them, and re-layouts  9.06 us (8%)
  matrix products  8.67 us (8%)
  other arithmetic  3.08 us (3%)
    ppermute x4, waiting for transfers between devices, partner(): lax.ppermute(array, axis, [(i, i ^ 1 << bit) for i in range(lax.axis_size...  35.6 us
    all_to_all x1, blocking collectives, per_device(): lax.all_to_all(outputs, 'head', split_axis=0, concat_axis=1, tiled=True)  22.9 us
    pallas_call x1, Pallas kernels, local_call(): pl.pallas_call(local_kernel, grid=(8 // HP,), in_specs=[wide, wide, wide,...  20.7 us
    ppermute x4, starting transfers between devices, partner(): lax.ppermute(array, axis, [(i, i ^ 1 << bit) for i in range(lax.axis_size...  9.84 us
    unnamed x11, local copies, waits for them, and re-layouts  4.66 us
    dot_general x3, matrix products, per_device(): joined = jnp.matmul(right_trans, left, preferred_element_type=F32)  4.22 us
    dot_general x4, matrix products, per_device(): both = jnp.matmul(prefix.astype(BF), other_b, preferred_element_type=F32)  3.16 us
  transfers between devices with their start and end apart: 4, of which 4 were waited for; matrix products, arithmetic and copies ran while one was open for 6% of the time, Pallas kernels for 0%

profile of v1, /device:TPU:1, one launch (start us, length us, event | category | flops | bytes accessed | tf_op | source)
XLA Modules:
  0.0 110.0 jit_solution(8645377822535547119)
XLA Ops:
  0.0 0.0 copy-start.3
  0.0 0.0 copy-start.1
  0.0 1.6 %copy.24.ld_ref = f32[512,8]{1,0:T(8,128)} copy(f32[512,8]{0,1:T(8,128)} %param.10) | data formatting | bytes 32768 | tf_op args[3]
  1.6 0.0 copy-start.2
  1.6 1.6 %copy.25.b_ref = f32[512,8]{1,0:T(8,128)} copy(f32[512,8]{0,1:T(8,128)} %param.11) | data formatting | bytes 32768 | tf_op args[4]
  3.2 20.7 %local_pass.1 = (f32[512,1024]{1,0:T(8,128)}, bf16[512,1024]{1,0:T(8,128)(2,1)}, f32[8,128,256]{2,1,0:T(8,128)}) custom-call(bf16[512,1024]{1,0:T(8,128)(2,1)} %q_ref.1, bf16[512,1024]{1,0:T(8,128)(2,1)} %k_ref.1, bf16[512,1024]{1,0:T(8,128)(2,1)} %v_ref.1, f32[512,8]{1,0:T(8,128)} %copy.24.ld_ref, f32[512,8]{1,0:T(8,128)} %copy.25.b_ref), custom_call_target="tpu_custom_call" | custom-call | tf_op jit(solution)/shard_map/local_pass/pallas_call | solution.py:182
  23.9 1.3 %convert_element_type.58 = bf16[8,128,256]{2,1,0:T(8,128)(2,1)S(1)} convert(f32[8,128,256]{2,1,0:T(8,128)} %get-tuple-element.9) | non-fusion elementwise | flops 262144 | bytes 1572864 | tf_op jit(solution)/shard_map/convert_element_type | solution.py:229
  25.2 2.5 %collective-permute-start = (bf16[8,128,256]{2,1,0:T(8,128)(2,1)S(1)}, bf16[8,128,256]{2,1,0:T(8,128)(2,1)S(1)}, u32[]{:S(2)}, u32[]{:S(2)}) collective-permute-start(bf16[8,128,256]{2,1,0:T(8,128)(2,1)S(1)} %convert_element_type.58), channel_id=1, source_target_pairs={{0,8},{8,0},{16,24},{24,16},{32,40},{40,32},{48,56},{56,48},{64,72... | collective-permute-start | bytes 1572872 | tf_op jit(solution)/shard_map/ppermute | solution.py:199
  27.7 11.6 %collective-permute-done = bf16[8,128,256]{2,1,0:T(8,128)(2,1)S(1)} collective-permute-done((bf16[8,128,256]{2,1,0:T(8,128)(2,1)S(1)}, bf16[8,128,256]{2,1,0:T(8,128)(2,1)S(1)}, u32[]{:S(2)}, u32[]{:S(2)}) %collective-permute-start) | collective-permute-done | bytes 524320 | tf_op jit(solution)/shard_map/ppermute | solution.py:199
  39.3 0.0 copy-start
  39.3 2.2 %fusion.40 = (bf16[8,128,256]{2,1,0:T(8,128)(2,1)}, f32[8,128,256]{2,1,0:T(8,128)}) fusion(f32[8,128,256]{2,1,0:T(8,128)} %get-tuple-element.9, bf16[8,128,256]{2,1,0:T(8,128)(2,1)S(1)} %collective-permute-done, pred[]{:T(512)S(6)} %eq.17, pred[256]{0:T(512)(128)(4,1)} %constant.18.clone.1, bf16[8,128,256]{2,1,0:T(8,128)(2,1)S(1)} %convert_element_type.58), kind=kOutput, calls=%fused_computation.57 | convolution fusion | flops 68812800 | bytes 4720384 | tf_op jit(solution)/shard_map/dot_general | solution.py:238
  41.5 3.1 %collective-permute-start.1 = (bf16[8,128,256]{2,1,0:T(8,128)(2,1)}, bf16[8,128,256]{2,1,0:T(8,128)(2,1)}, u32[]{:S(2)}, u32[]{:S(2)}) collective-permute-start(bf16[8,128,256]{2,1,0:T(8,128)(2,1)} %get-tuple-element.11), channel_id=1, source_target_pairs={{0,16},{8,24},{16,0},{24,8},{32,48},{40,56},{48,32},{56,40},{64,80... | collective-permute-start | bytes 1572872 | tf_op jit(solution)/shard_map/ppermute | solution.py:199
  44.6 0.0 copy-done.3
  44.6 1.5 %copy.38 = bf16[64,8,8,128]{3,2,1,0:T(8,128)(2,1)S(1)} copy(bf16[64,8,8,128]{3,1,2,0:T(8,128)(2,1)} %bitcast.28) | data formatting | bytes 2097152
  46.1 0.0 copy-done
  46.2 1.9 %copy.33 = f32[512,1024]{0,1:T(8,128)S(1)} copy(f32[512,1024]{1,0:T(8,128)} %get-tuple-element.8) | data formatting | bytes 4194304 | tf_op jit(solution)/shard_map/broadcast_in_dim;reshape | solution.py:212
  48.1 0.0 copy-done.1
  48.1 0.1 mul.24
  48.2 0.1 mul.25
  48.3 7.4 %collective-permute-done.1 = bf16[8,128,256]{2,1,0:T(8,128)(2,1)} collective-permute-done((bf16[8,128,256]{2,1,0:T(8,128)(2,1)}, bf16[8,128,256]{2,1,0:T(8,128)(2,1)}, u32[]{:S(2)}, u32[]{:S(2)}) %collective-permute-start.1) | collective-permute-done | bytes 524320 | tf_op jit(solution)/shard_map/ppermute | solution.py:199
  55.7 0.0 copy-done.2
  55.7 1.7 %fusion.41 = (bf16[8,128,256]{2,1,0:T(8,128)(2,1)S(1)}, f32[8,128,256]{2,1,0:T(8,128)S(1)}) fusion(f32[8,128,256]{2,1,0:T(8,128)} %get-tuple-element.12, bf16[8,128,256]{2,1,0:T(8,128)(2,1)} %collective-permute-done.1, pred[]{:T(512)S(6)} %eq.19, pred[256]{0:T(512)(128)(4,1)S(1)} %copy-done.2, bf16[8,128,256]{2,1,0:T(8,128)(2,1)} %get-tuple-element.11), kind=kOutput, calls=%fused_computation.58 | convolution fusion | flops 68812800 | bytes 4720384 | tf_op jit(solution)/shard_map/dot_general | solution.py:238
  57.5 1.3 %collective-permute-start.2 = (bf16[8,128,256]{2,1,0:T(8,128)(2,1)S(1)}, bf16[8,128,256]{2,1,0:T(8,128)(2,1)S(1)}, u32[]{:S(2)}, u32[]{:S(2)}) collective-permute-start(bf16[8,128,256]{2,1,0:T(8,128)(2,1)S(1)} %get-tuple-element.13), channel_id=1, source_target_pairs={{0,32},{8,40},{16,48},{24,56},{32,0},{40,8},{48,16},{56,24},{64,96... | collective-permute-start | bytes 1572872 | tf_op jit(solution)/shard_map/ppermute | solution.py:199
  58.8 1.3 %fusion.35 = bf16[8,128,256]{2,1,0:T(8,128)(2,1)S(1)} fusion(bf16[8,128,256]{2,1,0:T(8,128)(2,1)} %copy-done, bf16[128,128]{1,0:T(8,128)(2,1)S(1)} %fusion.38), kind=kOutput, calls=%fused_computation.49 | convolution fusion | flops 67108864 | bytes 1081344 | tf_op jit(solution)/shard_map/dot_general | solution.py:232
  60.1 0.1 fusion.19
  60.2 1.3 %fusion.17 = bf16[8,128,256]{2,1,0:T(8,128)(2,1)S(1)} fusion(bf16[8,128,256]{2,1,0:T(8,128)(2,1)} %collective-permute-done.1, bf16[8,128,256]{2,1,0:T(8,128)(2,1)S(1)} %fusion.35, bf16[128,128]{1,0:T(8,128)(2,1)S(1)} %fusion.37, pred[]{:T(512)S(6)} %eq.17), kind=kOutput, calls=%fused_computation.30 | convolution fusion | flops 67239936 | bytes 1343489 | tf_op jit(solution)/shard_map/dot_general | solution.py:232
  61.5 7.4 %collective-permute-done.2 = bf16[8,128,256]{2,1,0:T(8,128)(2,1)S(1)} collective-permute-done((bf16[8,128,256]{2,1,0:T(8,128)(2,1)S(1)}, bf16[8,128,256]{2,1,0:T(8,128)(2,1)S(1)}, u32[]{:S(2)}, u32[]{:S(2)}) %collective-permute-start.2) | collective-permute-done | bytes 524320 | tf_op jit(solution)/shard_map/ppermute | solution.py:199
  68.9 0.3 fusion.1
  69.2 2.9 %collective-permute-start.3 = (bf16[8,128,256]{2,1,0:T(8,128)(2,1)S(1)}, bf16[8,128,256]{2,1,0:T(8,128)(2,1)S(1)}, u32[]{:S(2)}, u32[]{:S(2)}) collective-permute-start(bf16[8,128,256]{2,1,0:T(8,128)(2,1)S(1)} %fusion.1), channel_id=1, source_target_pairs={{0,64},{8,72},{16,80},{24,88},{32,96},{40,104},{48,112},{56,120},{... | collective-permute-start | bytes 1572872 | tf_op jit(solution)/shard_map/ppermute | solution.py:199
  72.1 0.1 fusion.20
  72.1 0.3 fusion.27
  72.4 0.1 fusion.21
  72.5 9.1 %collective-permute-done.3 = bf16[8,128,256]{2,1,0:T(8,128)(2,1)S(1)} collective-permute-done((bf16[8,128,256]{2,1,0:T(8,128)(2,1)S(1)}, bf16[8,128,256]{2,1,0:T(8,128)(2,1)S(1)}, u32[]{:S(2)}, u32[]{:S(2)}) %collective-permute-start.3) | collective-permute-done | bytes 524320 | tf_op jit(solution)/shard_map/ppermute | solution.py:199
  81.6 0.2 fusion.3
  81.9 1.3 %convolution_bitcast_fusion = f32[512,8,4,128]{0,3,2,1:T(8,128)S(1)} fusion(bf16[512,8,128,1]{2,1,0,3:T(8,128)(2,1)S(1)} %bitcast.26, bf16[1,8,128,128]{3,2,1,0:T(8,128)(2,1)S(1)} %fusion.3, bf16[1,8,128,128]{3,2,1,0:T(8,128)(2,1)S(1)} %fusion.21, bf16[1,8,128,128]{3,2,1,0:T(8,128)(2,1)S(1)} %fusion.20, bf16[1,8,128,128]{3,2,1,0:T(8,128)(2,1)S(1)} %fusion.19), kind=kOutput, calls=%fused_computation.2 | convolution fusion | flops 538443776 | bytes 10485760 | tf_op jit(solution)/shard_map/thd,lhde->thle/dot_general | solution.py:203
  83.2 1.6 %fusion = bf16[512,8,128]{0,2,1:T(8,128)(2,1)S(1)} fusion(f32[512,8,4,128]{0,3,2,1:T(8,128)S(1)} %convolution_bitcast_fusion, f32[512,8,1,128]{0,3,2,1:T(8,128)S(1)} %bitcast.25, f32[512,8,5]{0,2,1:T(8,128)S(1)} %broadcast_multiply_fusion), kind=kLoop, calls=%fused_computation.1 | loop fusion | flops 7340032 | bytes 11616256 | tf_op jit(solution)/shard_map/reduce_sum | solution.py:217
  84.8 0.8 copy.29
  85.5 0.5 convert_element_type.69
  86.0 22.9 %all_to_all.16 = bf16[8,64,1024]{2,1,0:T(8,128)(2,1)S(1)} all-to-all(bf16[8,64,1024]{2,1,0:T(8,128)(2,1)S(1)} %convert_element_type.69), channel_id=1, replica_groups=mesh['ctx'=16,'head'=8] {'head'}, dimensions={0} | all-to-all | bytes 2097152 | tf_op jit(solution)/shard_map/all_to_all | solution.py:241
  108.9 1.1 copy.37
  (5 shorter events, 0.1 us)
Async XLA Ops:
  0.0 44.6 %copy-start.3 = (s32[8]{0:T(128)S(1)}, s32[8]{0:T(128)}, u32[]{:S(2)}) copy-start(s32[8]{0:T(128)} %param.13) | copy-start | bytes 100
  0.0 48.1 %copy-start.1 = (f32[512,40]{0,1:T(8,128)S(1)}, f32[512,40]{0,1:T(8,128)}, u32[]{:S(2)}) copy-start(f32[512,40]{0,1:T(8,128)} %param.12) | copy-start | bytes 245764
  1.6 54.1 %copy-start.2 = (pred[256]{0:T(512)(128)(4,1)S(1)}, pred[256]{0:T(512)(128)(4,1)}, u32[]{:S(2)}) copy-start(pred[256]{0:T(512)(128)(4,1)} %constant.18.clone.1) | copy-start | bytes 772
  25.2 14.2 %collective-permute-start = (bf16[8,128,256]{2,1,0:T(8,128)(2,1)S(1)}, bf16[8,128,256]{2,1,0:T(8,128)(2,1)S(1)}, u32[]{:S(2)}, u32[]{:S(2)}) collective-permute-start(bf16[8,128,256]{2,1,0:T(8,128)(2,1)S(1)} %convert_element_type.58), channel_id=1, source_target_pairs={{0,8},{8,0},{16,24},{24,16},{32,40},{40,32},{48,56},{56,48},{64,72... | collective-permute-start | bytes 1572872 | tf_op jit(solution)/shard_map/ppermute | solution.py:199
  39.3 6.8 %copy-start = (bf16[8,128,256]{2,1,0:T(8,128)(2,1)}, bf16[8,128,256]{2,1,0:T(8,128)(2,1)S(1)}, u32[]{:S(2)}) copy-start(bf16[8,128,256]{2,1,0:T(8,128)(2,1)S(1)} %collective-permute-done) | copy-start | bytes 1572868
  41.5 14.2 %collective-permute-start.1 = (bf16[8,128,256]{2,1,0:T(8,128)(2,1)}, bf16[8,128,256]{2,1,0:T(8,128)(2,1)}, u32[]{:S(2)}, u32[]{:S(2)}) collective-permute-start(bf16[8,128,256]{2,1,0:T(8,128)(2,1)} %get-tuple-element.11), channel_id=1, source_target_pairs={{0,16},{8,24},{16,0},{24,8},{32,48},{40,56},{48,32},{56,40},{64,80... | collective-permute-start | bytes 1572872 | tf_op jit(solution)/shard_map/ppermute | solution.py:199
  57.5 11.4 %collective-permute-start.2 = (bf16[8,128,256]{2,1,0:T(8,128)(2,1)S(1)}, bf16[8,128,256]{2,1,0:T(8,128)(2,1)S(1)}, u32[]{:S(2)}, u32[]{:S(2)}) collective-permute-start(bf16[8,128,256]{2,1,0:T(8,128)(2,1)S(1)} %get-tuple-element.13), channel_id=1, source_target_pairs={{0,32},{8,40},{16,48},{24,56},{32,0},{40,8},{48,16},{56,24},{64,96... | collective-permute-start | bytes 1572872 | tf_op jit(solution)/shard_map/ppermute | solution.py:199
  69.2 12.4 %collective-permute-start.3 = (bf16[8,128,256]{2,1,0:T(8,128)(2,1)S(1)}, bf16[8,128,256]{2,1,0:T(8,128)(2,1)S(1)}, u32[]{:S(2)}, u32[]{:S(2)}) collective-permute-start(bf16[8,128,256]{2,1,0:T(8,128)(2,1)S(1)} %fusion.1), channel_id=1, source_target_pairs={{0,64},{8,72},{16,80},{24,88},{32,96},{40,104},{48,112},{56,120},{... | collective-permute-start | bytes 1572872 | tf_op jit(solution)/shard_map/ppermute | solution.py:199

commit v2 on v1

--- a/solution.py
+++ b/solution.py
@@ -74,15 +74,17 @@
     return [x.astype(F32) + dotf(x, e) for x, e in zip(inv_b, errs)]
 
 
-def setup_gates(decay, rate, g_ref, gt_ref, bt_ref):
+def setup_gates(decay_t, rate_t, g_ref, b_ref, gt_ref):
     ii = lax.broadcasted_iota(jnp.int32, (C, C), 0)
     jj = lax.broadcasted_iota(jnp.int32, (C, C), 1)
-    tri = (ii >= jj).astype(F32)
+    tri = (ii <= jj).astype(F32)
     for c in range(NCH):
         sl = slice(c * C, (c + 1) * C)
-        g_ref[sl, :] = jnp.dot(tri, decay[sl, :], precision=lax.Precision.HIGHEST, preferred_element_type=F32)
-    gt_ref[...] = g_ref[...].T
-    bt_ref[...] = rate.T
+        gt_ref[:, sl] = jnp.dot(
+            decay_t[:, sl], tri, precision=lax.Precision.HIGHEST, preferred_element_type=F32
+        )
+    g_ref[...] = gt_ref[...].T
+    b_ref[...] = rate_t.T
 
 
 def local_heads(heads, q, k, v, g_all, b_all, gt_ref, bt_ref):
@@ -154,12 +156,12 @@
     return near, rows, pair
 
 
-def local_kernel(q_ref, k_ref, v_ref, ld_ref, b_ref, near_ref, rows_ref, run_ref, g_ref, gt_ref, bt_ref):
+def local_kernel(q_ref, k_ref, v_ref, ldt_ref, bt_ref, near_ref, rows_ref, run_ref, g_ref, b_ref, gt_ref):
     p = pl.program_id(0)
 
     @pl.when(p == 0)
     def _():
-        setup_gates(ld_ref[...], b_ref[...], g_ref, gt_ref, bt_ref)
+        setup_gates(ldt_ref[...], bt_ref[...], g_ref, b_ref, gt_ref)
 
     heads = [p * HP + n for n in range(HP)]
 
@@ -177,7 +179,7 @@
 
 def local_call(q, k, v, decay, rate):
     wide = pl.BlockSpec((512, HP * 128), lambda p: (0, p))
-    gate = pl.BlockSpec((512, 8), lambda p: (0, 0))
+    gate = pl.BlockSpec((8, 512), lambda p: (0, 0))
     run = pl.BlockSpec((HP, 128, 256), lambda p: (p, 0, 0))
     return pl.pallas_call(
         local_kernel,
@@ -189,56 +191,182 @@
             jax.ShapeDtypeStruct((512, 1024), BF),
             jax.ShapeDtypeStruct((8, 128, 256), F32),
         ],
-        scratch_shapes=[pltpu.VMEM((512, 8), F32), pltpu.VMEM((8, 512), F32), pltpu.VMEM((8, 512), F32)],
+        scratch_shapes=[pltpu.VMEM((512, 8), F32), pltpu.VMEM((512, 8), F32), pltpu.VMEM((8, 512), F32)],
         compiler_params=pltpu.CompilerParams(vmem_limit_bytes=56 << 20),
         name="local_pass",
-    )(q, k, v, decay, rate)
-
-
-def partner(array, axis, bit):
-    return lax.ppermute(array, axis, [(i, i ^ 1 << bit) for i in range(lax.axis_size(axis))])
-
-
-def low_product(form, left_op, right_op):
-    return jnp.einsum(form, left_op, right_op, preferred_element_type=F32)
-
-
-def finish(near, rows, carried, weights, levels_in):
-    length, wide = near.shape
-    head_count = wide // 128
-    near_part = near.reshape(length, head_count, 128)
-    row_part = rows.reshape(length, head_count, 128)
-    far_part = low_product("thd,lhde->thle", row_part, carried.astype(BF))
-    terms = jnp.concatenate([near_part[:, :, None], far_part], axis=2)
-    level_ids = jnp.arange(LEVELS)
-    keep_mask = (level_ids[None, :] < levels_in[:, None]).astype(weights.dtype)
-    scaled = weights.reshape(length // BLOCK, BLOCK, head_count, LEVELS) * keep_mask[:, None, None, :]
-    scaled = scaled.reshape(length, head_count, LEVELS)
-    total = jnp.sum(scaled[..., None] * terms, axis=2)
-    return total.astype(BF).reshape(length, wide)
+    )(q, k, v, decay.T, rate.T)
+
+
+MESH = pl.DeviceIdType.MESH
+HEADS = 8
+LEV = 4
+
+
+def exchange_kernel(
+    near_ref, rows_ref, run_ref, wt_ref, lev_ref, out_ref,
+    sent, got, sent_s, got_s, run_f, prefix, carried, w_ref, stage,
+    send_sem, recv_sem, out_send, out_recv, own_sem,
+):
+    pos = lax.axis_index("ctx")
+    me = lax.axis_index("head")
+    bits = [(pos // 2**r) % 2 for r in range(LEV)]
+    mates = [pos + (1 - 2 * bits[r]) * 2**r for r in range(LEV)]
+    peers = [lax.rem(me + d, HEADS) for d in range(1, HEADS)]
+
+    barrier = pltpu.get_barrier_semaphore()
+    for m in mates:
+        pl.semaphore_signal(barrier, inc=1, device_id={"ctx": m}, device_id_type=MESH)
+    for j in peers:
+        pl.semaphore_signal(barrier, inc=1, device_id={"head": j}, device_id_type=MESH)
+    pl.semaphore_wait(barrier, LEV + HEADS - 1)
+
+    def run_copy(r, h):
+        if r == LEV - 1:
+            src, dst = sent_s.at[h], got_s.at[h]
+        else:
+            src, dst = sent.at[r, h], got.at[r, h]
+        return pltpu.make_async_remote_copy(
+            src_ref=src,
+            dst_ref=dst,
+            send_sem=send_sem.at[r, h],
+            recv_sem=recv_sem.at[r, h],
+            device_id={"ctx": mates[r]},
+            device_id_type=MESH,
+        )
+
+    def head_cols(h):
+        return pl.ds(pl.multiple_of(h * 128, 128), 128)
+
+    def out_copy(h, src_dev, dst_dev):
+        cols = pl.ds(pl.multiple_of(src_dev * 1024 + h * 128, 128), 128)
+        return pltpu.make_async_remote_copy(
+            src_ref=stage.at[pl.ds(pl.multiple_of(dst_dev * 64, 64), 64), head_cols(h)],
+            dst_ref=out_ref.at[:, cols],
+            send_sem=out_send.at[h, dst_dev],
+            recv_sem=out_recv.at[h, src_dev],
+            device_id={"head": dst_dev},
+            device_id_type=MESH,
+        )
+
+    def own_copy(h):
+        cols = pl.ds(pl.multiple_of(me * 1024 + h * 128, 128), 128)
+        return pltpu.make_async_copy(
+            stage.at[pl.ds(pl.multiple_of(me * 64, 64), 64), head_cols(h)], out_ref.at[:, cols], own_sem.at[h]
+        )
+
+    @pl.loop(0, HEADS)
+    def _(h):
+        sent[0, h] = run_ref[h].astype(BF)
+        run_copy(0, h).start()
+
+    lane = lax.broadcasted_iota(jnp.int32, (64, 40), 1)
+    level = lane
+    for m in range(1, HEADS):
+        level = jnp.where(lane >= LEVELS * m, lane - LEVELS * m, level)
+    w_all = wt_ref[...].T
+    for n in range(8):
+        sl = slice(64 * n, 64 * n + 64)
+        w_ref[sl, :] = jnp.where(level < lev_ref[n], w_all[sl], 0.0)
+
+    lanes = lax.broadcasted_iota(jnp.int32, (512, 40), 1)
+
+    def finish(h):
+        w = w_ref[...]
+        weight = [
+            jnp.sum(jnp.where(lanes == h * LEVELS + i, w, 0.0), axis=1, keepdims=True) for i in range(LEVELS)
+        ]
+        far = dotf(rows_ref[:, head_cols(h)], carried[h])
+        total = weight[0] * near_ref[:, head_cols(h)]
+        for i in range(LEV):
+            total = total + weight[i + 1] * far[:, i * 128 : (i + 1) * 128]
+        stage[:, head_cols(h)] = total.astype(BF)
+        for j in peers:
+            out_copy(h, me, j).start()
+        own_copy(h).start()
+
+    for r in range(LEV):
+        up = bits[r] == 1
+
+        @pl.loop(0, HEADS)
+        def _(h):
+            run_copy(r, h).wait_recv()
+            cr = slice(r * 128, (r + 1) * 128)
+            if r == LEV - 1:
+                other = got_s[h]
+                far = dotf(prefix[h].astype(BF), other)
+                carried[h, :, cr] = jnp.where(up, far, 0.0).astype(BF)
+                finish(h)
+                return
+            other = got[r, h]
+            own_b = sent[r, h]
+            other_f = other.astype(F32)
+            own_f = run_ref[h] if r == 0 else run_f[h]
+            left = jnp.where(up, other_f, own_b.astype(F32)).astype(BF)
+            right_t = jnp.where(up, own_b[:, 128:].astype(F32), other_f[:, 128:]).astype(BF)
+            right_s = jnp.where(up, own_f[:, :128], other_f[:, :128])
+            if r == 0:
+                ii = lax.broadcasted_iota(jnp.int32, (128, 128), 0)
+                jj = lax.broadcasted_iota(jnp.int32, (128, 128), 1)
+                both = other_f
+                old = (ii == jj).astype(F32)
+            else:
+                old = prefix[h]
+                both = dotf(old.astype(BF), left)
+            carried[h, :, cr] = jnp.where(up, both[:, :128], 0.0).astype(BF)
+            prefix[h] = jnp.where(up, both[:, 128:], old)
+            if r < LEV - 2:
+                joined = dotf(right_t, left)
+                joined = jnp.concatenate([joined[:, :128] + right_s, joined[:, 128:]], axis=1)
+                run_f[h] = joined
+                sent[r + 1, h] = joined.astype(BF)
+            else:
+                sent_s[h] = (dotf(right_t, left[:, :128]) + right_s).astype(BF)
+            run_copy(r + 1, h).start()
+
+    @pl.loop(0, HEADS)
+    def _(h):
+        for r in range(LEV):
+            run_copy(r, h).wait_send()
+        own_copy(h).wait()
+        for j in peers:
+            out_copy(h, me, j).wait_send()
+        for j in peers:
+            out_copy(h, j, me).wait_recv()
+
+
+def exchange_call(near, rows, run, weights, levels_in):
+    vmem = pl.BlockSpec(memory_space=pltpu.VMEM)
+    return pl.pallas_call(
+        exchange_kernel,
+        in_specs=[vmem, vmem, vmem, vmem, pl.BlockSpec(memory_space=pltpu.SMEM)],
+        out_specs=pl.BlockSpec(memory_space=pl.ANY),
+        out_shape=jax.ShapeDtypeStruct((64, 8192), BF),
+        scratch_shapes=[
+            pltpu.VMEM((LEV - 1, HEADS, 128, 256), BF),
+            pltpu.VMEM((LEV - 1, HEADS, 128, 256), BF),
+            pltpu.VMEM((HEADS, 128, 128), BF),
+            pltpu.VMEM((HEADS, 128, 128), BF),
+            pltpu.VMEM((HEADS, 128, 256), F32),
+            pltpu.VMEM((HEADS, 128, 128), F32),
+            pltpu.VMEM((HEADS, 128, LEV * 128), BF),
+            pltpu.VMEM((512, 40), F32),
+            pltpu.VMEM((512, 1024), BF),
+            pltpu.SemaphoreType.DMA((LEV, HEADS)),
+            pltpu.SemaphoreType.DMA((LEV, HEADS)),
+            pltpu.SemaphoreType.DMA((HEADS, HEADS)),
+            pltpu.SemaphoreType.DMA((HEADS, HEADS)),
+            pltpu.SemaphoreType.DMA((HEADS,)),
+        ],
+        compiler_params=pltpu.CompilerParams(
+            collective_id=0, has_side_effects=True, vmem_limit_bytes=56 << 20
+        ),
+        name="exchange",
+    )(near, rows, run, weights.T, levels_in)
 
 
 def per_device(queries, key_rows, value_rows, log_decay, write_rate, level_weights, block_levels):
-    near, rows, own = local_call(queries, key_rows, value_rows, log_decay, write_rate)
-    bits_total = lax.axis_size("ctx").bit_length() - 1
-    position = lax.axis_index("ctx")
-    prefix = jnp.broadcast_to(jnp.eye(128, dtype=F32), (8, 128, 128))
-    carried = []
-    for section in range(bits_total):
-        upper = position >> section & 1 == 1
-        own_b = own.astype(BF)
-        other_b = partner(own_b, "ctx", section)
-        left = jnp.where(upper, other_b, own_b)
-        both = jnp.matmul(prefix.astype(BF), other_b, preferred_element_type=F32)
-        carried.append(jnp.where(upper, both[..., :128], 0.0))
-        prefix = jnp.where(upper, both[..., 128:], prefix)
-        if section + 1 < bits_total:
-            right_trans = jnp.where(upper, own_b, other_b)[..., 128:]
-            right_state = jnp.where(upper, own, other_b.astype(F32))[..., :128]
-            joined = jnp.matmul(right_trans, left, preferred_element_type=F32)
-            own = joined + jnp.concatenate([right_state, jnp.zeros_like(right_state)], axis=-1)
-    outputs = finish(near, rows, jnp.stack(carried, axis=0), level_weights, block_levels)
-    return lax.all_to_all(outputs, "head", split_axis=0, concat_axis=1, tiled=True)
+    near, rows, run = local_call(queries, key_rows, value_rows, log_decay, write_rate)
+    return exchange_call(near, rows, run, level_weights, block_levels)
 
 
 def solution(mesh):

time: 110 us -> 77.5 us (0.70)
  Pallas kernels: 20.7 us -> 75.1 us
  waiting for transfers between devices: 35.6 us -> 0 us
  blocking collectives: 22.9 us -> 0 us
  starting transfers between devices: 9.84 us -> 0 us
  matrix products: 8.67 us -> 0 us
  local copies, waits for them, and re-layouts: 9.06 us -> 2.26 us
  other arithmetic: 3.08 us -> 0 us
    pallas_call x0 -> x1, Pallas kernels: none -> 54.6 us  [exchange_call(): pl.pallas_call(exchange_kernel, in_specs=[vmem, vmem, vmem, vmem, pl.Bloc...]
    ppermute x4 -> x0, waiting for transfers between devices: 35.6 us -> none  [partner(): lax.ppermute(array, axis, [(i, i ^ 1 << bit) for i in range(lax.axis_size...]
    all_to_all x1 -> x0, blocking collectives: 22.9 us -> none  [per_device(): lax.all_to_all(outputs, 'head', split_axis=0, concat_axis=1, tiled=True)]
    ppermute x4 -> x0, starting transfers between devices: 9.84 us -> none  [partner(): lax.ppermute(array, axis, [(i, i ^ 1 << bit) for i in range(lax.axis_size...]
    dot_general x8 -> x0, matrix products: 8.67 us -> none  [the longest x3 4.22 us: per_device(): joined = jnp.matmul(right_trans, left, preferred_element_type=F32)]
    unnamed x11 -> x1, local copies, waits for them, and re-layouts: 4.66 us -> 2.26 us
    another operation x1 -> x0, local copies, waits for them, and re-layouts: 1.93 us -> none  [finish(): terms = jnp.concatenate([near_part[:, :, None], far_part], axis=2)]
    reduce_sum x1 -> x0, other arithmetic: 1.59 us -> none  [finish(): total = jnp.sum(scaled[..., None] * terms, axis=2)]
  transfers between devices with their start and end apart: 4 -> 0, of which waited for: 4 -> 0; matrix products, arithmetic and copies ran while one was open for 6% -> 0% of each run, Pallas kernels for 0% -> 0%
where the time goes in v2:
time: 77.5 us; the launch traced here: 77.3 us
  Pallas kernels  75.1 us (97%)
  local copies, waits for them, and re-layouts  2.26 us (3%)
    pallas_call x1, Pallas kernels, exchange_call(): pl.pallas_call(exchange_kernel, in_specs=[vmem, vmem, vmem, vmem, pl.Bloc...  54.6 us
    pallas_call x1, Pallas kernels, local_call(): pl.pallas_call(local_kernel, grid=(8 // HP,), in_specs=[wide, wide, wide,...  20.5 us
    unnamed x1, local copies, waits for them, and re-layouts  2.26 us

profile of v2, /device:TPU:1, one launch (start us, length us, event | category | flops | bytes accessed | tf_op | source)
XLA Modules:
  0.0 77.3 jit_solution(9053560076647723711)
XLA Ops:
  0.0 20.5 %local_pass.1 = (f32[512,1024]{1,0:T(8,128)}, bf16[512,1024]{1,0:T(8,128)(2,1)}, f32[8,128,256]{2,1,0:T(8,128)}) custom-call(bf16[512,1024]{1,0:T(8,128)(2,1)} %q_ref.1, bf16[512,1024]{1,0:T(8,128)(2,1)} %k_ref.1, bf16[512,1024]{1,0:T(8,128)(2,1)} %v_ref.1, f32[8,512]{1,0:T(8,128)} %bitcast.4, f32[8,512]{1,0:T(8,128)} %bitcast.5), custom_call_target="tpu_custom_call" | custom-call | tf_op jit(solution)/shard_map/local_pass/pallas_call | solution.py:184
  20.5 54.6 %exchange.1 = bf16[64,8192]{1,0:T(8,128)(2,1)} custom-call(f32[512,1024]{1,0:T(8,128)} %get-tuple-element.8.near_ref, bf16[512,1024]{1,0:T(8,128)(2,1)} %get-tuple-element.9.rows_ref, f32[8,128,256]{2,1,0:T(8,128)} %get-tuple-element.10.run_ref, f32[40,512]{1,0:T(8,128)} %bitcast.3, s32[8]{0:T(128)} %lev_ref.1), custom_call_target="tpu_custom_call" | custom-call | tf_op jit(solution)/shard_map/exchange/pallas_call | solution.py:339
  75.1 2.3 %copy.9 = bf16[64,8192]{1,0:T(8,128)(2,1)} copy(bf16[64,8192]{1,0:T(8,128)(2,1)} %exchange.1) | data formatting | bytes 2097152

commit v3 on v2

--- a/solution.py
+++ b/solution.py
@@ -156,56 +156,16 @@
     return near, rows, pair
 
 
-def local_kernel(q_ref, k_ref, v_ref, ldt_ref, bt_ref, near_ref, rows_ref, run_ref, g_ref, b_ref, gt_ref):
-    p = pl.program_id(0)
-
-    @pl.when(p == 0)
-    def _():
-        setup_gates(ldt_ref[...], bt_ref[...], g_ref, b_ref, gt_ref)
-
-    heads = [p * HP + n for n in range(HP)]
-
-    def cut(ref):
-        return [ref[:, n * 128 : (n + 1) * 128] for n in range(HP)]
-
-    near, rows, pair = local_heads(
-        heads, cut(q_ref), cut(k_ref), cut(v_ref), g_ref[...], b_ref[...], gt_ref, bt_ref
-    )
-    for n in range(HP):
-        near_ref[:, n * 128 : (n + 1) * 128] = near[n]
-        rows_ref[:, n * 128 : (n + 1) * 128] = rows[n]
-        run_ref[n] = pair[n]
-
-
-def local_call(q, k, v, decay, rate):
-    wide = pl.BlockSpec((512, HP * 128), lambda p: (0, p))
-    gate = pl.BlockSpec((8, 512), lambda p: (0, 0))
-    run = pl.BlockSpec((HP, 128, 256), lambda p: (p, 0, 0))
-    return pl.pallas_call(
-        local_kernel,
-        grid=(8 // HP,),
-        in_specs=[wide, wide, wide, gate, gate],
-        out_specs=[wide, wide, run],
-        out_shape=[
-            jax.ShapeDtypeStruct((512, 1024), F32),
-            jax.ShapeDtypeStruct((512, 1024), BF),
-            jax.ShapeDtypeStruct((8, 128, 256), F32),
-        ],
-        scratch_shapes=[pltpu.VMEM((512, 8), F32), pltpu.VMEM((512, 8), F32), pltpu.VMEM((8, 512), F32)],
-        compiler_params=pltpu.CompilerParams(vmem_limit_bytes=56 << 20),
-        name="local_pass",
-    )(q, k, v, decay.T, rate.T)
-
-
 MESH = pl.DeviceIdType.MESH
 HEADS = 8
 LEV = 4
 
 
-def exchange_kernel(
-    near_ref, rows_ref, run_ref, wt_ref, lev_ref, out_ref,
-    sent, got, sent_s, got_s, run_f, prefix, carried, w_ref, stage,
-    send_sem, recv_sem, out_send, out_recv, own_sem,
+def fused_kernel(
+    q_hbm, k_hbm, v_hbm, ldt_ref, bt_ref, wt_ref, lev_ref, out_ref,
+    q_ref, k_ref, v_ref, g_ref, b_ref, gt_ref, near_ref, rows_ref,
+    box, box_s, run_f, prefix, carried, w_ref, stage,
+    in_sem, send_sem, recv_sem, out_send, out_recv, own_sem,
 ):
     pos = lax.axis_index("ctx")
     me = lax.axis_index("head")
@@ -218,13 +178,23 @@
         pl.semaphore_signal(barrier, inc=1, device_id={"ctx": m}, device_id_type=MESH)
     for j in peers:
         pl.semaphore_signal(barrier, inc=1, device_id={"head": j}, device_id_type=MESH)
-    pl.semaphore_wait(barrier, LEV + HEADS - 1)
+
+    def in_copies(p):
+        cols = pl.ds(pl.multiple_of(p * HP * 128, HP * 128), HP * 128)
+        return [
+            pltpu.make_async_copy(src.at[:, cols], dst.at[:, cols], in_sem.at[i, p])
+            for i, (src, dst) in enumerate(((k_hbm, k_ref), (q_hbm, q_ref), (v_hbm, v_ref)))
+        ]
+
+    for p in range(HEADS // HP):
+        for c in in_copies(p):
+            c.start()
 
     def run_copy(r, h):
         if r == LEV - 1:
-            src, dst = sent_s.at[h], got_s.at[h]
+            src, dst = box_s.at[h, 0], box_s.at[h, 1]
         else:
-            src, dst = sent.at[r, h], got.at[r, h]
+            src, dst = box.at[r, h, 0], box.at[r, h, 1]
         return pltpu.make_async_remote_copy(
             src_ref=src,
             dst_ref=dst,
@@ -254,10 +224,7 @@
             stage.at[pl.ds(pl.multiple_of(me * 64, 64), 64), head_cols(h)], out_ref.at[:, cols], own_sem.at[h]
         )
 
-    @pl.loop(0, HEADS)
-    def _(h):
-        sent[0, h] = run_ref[h].astype(BF)
-        run_copy(0, h).start()
+    setup_gates(ldt_ref[...], bt_ref[...], g_ref, b_ref, gt_ref)
 
     lane = lax.broadcasted_iota(jnp.int32, (64, 40), 1)
     level = lane
@@ -284,44 +251,72 @@
             out_copy(h, me, j).start()
         own_copy(h).start()
 
-    for r in range(LEV):
+    def step(r, h):
         up = bits[r] == 1
-
-        @pl.loop(0, HEADS)
+        run_copy(r, h).wait_recv()
+        cr = slice(r * 128, (r + 1) * 128)
+        if r == LEV - 1:
+            far = dotf(prefix[h].astype(BF), box_s[h, 1])
+            carried[h, :, cr] = jnp.where(up, far, 0.0).astype(BF)
+            finish(h)
+            return
+        left = box[r, h, bits[r]]
+        right = box[r, h, 1 - bits[r]]
+        right_s = jnp.where(up, run_f[h, :, :128], right[:, :128].astype(F32))
+        if r == 0:
+            ii = lax.broadcasted_iota(jnp.int32, (128, 128), 0)
+            jj = lax.broadcasted_iota(jnp.int32, (128, 128), 1)
+            both = left.astype(F32)
+            old = (ii == jj).astype(F32)
+        else:
+            old = prefix[h]
+            both = dotf(old.astype(BF), left)
+        carried[h, :, cr] = jnp.where(up, both[:, :128], 0.0).astype(BF)
+        prefix[h] = jnp.where(up, both[:, 128:], old)
+        if r < LEV - 2:
+            joined = dotf(right[:, 128:], left)
+            state = joined[:, :128] + right_s
+            run_f[h] = state
+            box[r + 1, h, 0, :, :128] = state.astype(BF)
+            box[r + 1, h, 0, :, 128:] = joined[:, 128:].astype(BF)
+        else:
+            box_s[h, 0] = (dotf(right[:, 128:], left[:, :128]) + right_s).astype(BF)
+        run_copy(r + 1, h).start()
+
+    def steps(r, lo, hi):
+        @pl.loop(lo, hi)
         def _(h):
-            run_copy(r, h).wait_recv()
-            cr = slice(r * 128, (r + 1) * 128)
-            if r == LEV - 1:
-                other = got_s[h]
-                far = dotf(prefix[h].astype(BF), other)
-                carried[h, :, cr] = jnp.where(up, far, 0.0).astype(BF)
-                finish(h)
-                return
-            other = got[r, h]
-            own_b = sent[r, h]
-            other_f = other.astype(F32)
-            own_f = run_ref[h] if r == 0 else run_f[h]
-            left = jnp.where(up, other_f, own_b.astype(F32)).astype(BF)
-            right_t = jnp.where(up, own_b[:, 128:].astype(F32), other_f[:, 128:]).astype(BF)
-            right_s = jnp.where(up, own_f[:, :128], other_f[:, :128])
-            if r == 0:
-                ii = lax.broadcasted_iota(jnp.int32, (128, 128), 0)
-                jj = lax.broadcasted_iota(jnp.int32, (128, 128), 1)
-                both = other_f
-                old = (ii == jj).astype(F32)
-            else:
-                old = prefix[h]
-                both = dotf(old.astype(BF), left)
-            carried[h, :, cr] = jnp.where(up, both[:, :128], 0.0).astype(BF)
-            prefix[h] = jnp.where(up, both[:, 128:], old)
-            if r < LEV - 2:
-                joined = dotf(right_t, left)
-                joined = jnp.concatenate([joined[:, :128] + right_s, joined[:, 128:]], axis=1)
-                run_f[h] = joined
-                sent[r + 1, h] = joined.astype(BF)
-            else:
-                sent_s[h] = (dotf(right_t, left[:, :128]) + right_s).astype(BF)
-            run_copy(r + 1, h).start()
+            step(r, h)
+
+    pairs = HEADS // HP
+
+    @pl.loop(0, pairs)
+    def _(p):
+        for c in in_copies(p):
+            c.wait()
+        heads = [p * HP + n for n in range(HP)]
+
+        def cut(ref):
+            return [ref[:, head_cols(h)] for h in heads]
+
+        near, rows, pair = local_heads(heads, cut(q_ref), cut(k_ref), cut(v_ref), g_ref[...], b_ref[...], gt_ref, bt_ref)
+
+        @pl.when(p == 0)
+        def _():
+            pl.semaphore_wait(barrier, LEV + HEADS - 1)
+
+        for n, h in enumerate(heads):
+            run_f[h] = pair[n][:, :128]
+            box[0, h, 0] = pair[n].astype(BF)
+            run_copy(0, h).start()
+        for n, h in enumerate(heads):
+            near_ref[:, head_cols(h)] = near[n]
+            rows_ref[:, head_cols(h)] = rows[n]
+        for r in range(LEV - 1):
+            steps(r, HP * jnp.maximum(p - 1 - r, 0), HP * jnp.maximum(p - r, 0))
+
+    for r, p in ((1, 2), (2, 1), (0, 3), (3, 0), (2, 2), (1, 3), (3, 1), (2, 3), (3, 2), (3, 3)):
+        steps(r, HP * p, HP * p + HP)
 
     @pl.loop(0, HEADS)
     def _(h):
@@ -334,23 +329,31 @@
             out_copy(h, j, me).wait_recv()
 
 
-def exchange_call(near, rows, run, weights, levels_in):
+def fused_call(q, k, v, decay, rate, weights, levels_in):
     vmem = pl.BlockSpec(memory_space=pltpu.VMEM)
+    hbm = pl.BlockSpec(memory_space=pl.ANY)
     return pl.pallas_call(
-        exchange_kernel,
-        in_specs=[vmem, vmem, vmem, vmem, pl.BlockSpec(memory_space=pltpu.SMEM)],
-        out_specs=pl.BlockSpec(memory_space=pl.ANY),
+        fused_kernel,
+        in_specs=[hbm, hbm, hbm, vmem, vmem, vmem, pl.BlockSpec(memory_space=pltpu.SMEM)],
+        out_specs=hbm,
         out_shape=jax.ShapeDtypeStruct((64, 8192), BF),
         scratch_shapes=[
-            pltpu.VMEM((LEV - 1, HEADS, 128, 256), BF),
-            pltpu.VMEM((LEV - 1, HEADS, 128, 256), BF),
-            pltpu.VMEM((HEADS, 128, 128), BF),
-            pltpu.VMEM((HEADS, 128, 128), BF),
-            pltpu.VMEM((HEADS, 128, 256), F32),
+            pltpu.VMEM((512, 1024), BF),
+            pltpu.VMEM((512, 1024), BF),
+            pltpu.VMEM((512, 1024), BF),
+            pltpu.VMEM((512, 8), F32),
+            pltpu.VMEM((512, 8), F32),
+            pltpu.VMEM((8, 512), F32),
+            pltpu.VMEM((512, 1024), F32),
+            pltpu.VMEM((512, 1024), BF),
+            pltpu.VMEM((LEV - 1, HEADS, 2, 128, 256), BF),
+            pltpu.VMEM((HEADS, 2, 128, 128), BF),
+            pltpu.VMEM((HEADS, 128, 128), F32),
             pltpu.VMEM((HEADS, 128, 128), F32),
             pltpu.VMEM((HEADS, 128, LEV * 128), BF),
             pltpu.VMEM((512, 40), F32),
             pltpu.VMEM((512, 1024), BF),
+            pltpu.SemaphoreType.DMA((3, HEADS // HP)),
             pltpu.SemaphoreType.DMA((LEV, HEADS)),
             pltpu.SemaphoreType.DMA((LEV, HEADS)),
             pltpu.SemaphoreType.DMA((HEADS, HEADS)),
@@ -360,16 +363,11 @@
         compiler_params=pltpu.CompilerParams(
             collective_id=0, has_side_effects=True, vmem_limit_bytes=56 << 20
         ),
-        name="exchange",
-    )(near, rows, run, weights.T, levels_in)
-
-
-def per_device(queries, key_rows, value_rows, log_decay, write_rate, level_weights, block_levels):
-    near, rows, run = local_call(queries, key_rows, value_rows, log_decay, write_rate)
-    return exchange_call(near, rows, run, level_weights, block_levels)
+        name="fused",
+    )(q, k, v, decay.T, rate.T, weights.T, levels_in)
 
 
 def solution(mesh):
     in_specs = (P("ctx", "head"),) * 6 + (P("ctx"),)
     out_specs = P(("ctx", "head"), None)
-    return jax.shard_map(per_device, mesh=mesh, in_specs=in_specs, out_specs=out_specs, check_vma=False)
+    return jax.shard_map(fused_call, mesh=mesh, in_specs=in_specs, out_specs=out_specs, check_vma=False)

time: 77.5 us -> 59.7 us (0.77)
  Pallas kernels: 75.1 us -> 57.2 us
    pallas_call x2 -> x1, Pallas kernels: 75.1 us -> 57.2 us  [fused_call(): pl.pallas_call(fused_kernel, in_specs=[hbm, hbm, hbm, vmem, vmem, vmem, p...]
where the time goes in v3:
time: 59.7 us; the launch traced here: 59.5 us
  Pallas kernels  57.2 us (96%)
  local copies, waits for them, and re-layouts  2.26 us (4%)
    pallas_call x1, Pallas kernels, fused_call(): pl.pallas_call(fused_kernel, in_specs=[hbm, hbm, hbm, vmem, vmem, vmem, p...  57.2 us
    unnamed x1, local copies, waits for them, and re-layouts  2.26 us

profile of v3, /device:TPU:1, one launch (start us, length us, event | category | flops | bytes accessed | tf_op | source)
XLA Modules:
  0.0 59.5 jit_solution(7312239754362284875)
XLA Ops:
  0.0 57.2 %fused.1 = bf16[64,8192]{1,0:T(8,128)(2,1)} custom-call(bf16[512,1024]{1,0:T(8,128)(2,1)} %q_hbm.1, bf16[512,1024]{1,0:T(8,128)(2,1)} %k_hbm.1, bf16[512,1024]{1,0:T(8,128)(2,1)} %v_hbm.1, f32[8,512]{1,0:T(8,128)} %bitcast.4, f32[8,512]{1,0:T(8,128)} %bitcast.5, f32[40,512]{1,0:T(8,128)} %bitcast.3, s32[8]{0:T(128)} %lev_ref.1), custom_call_target="tpu_custom_call" | custom-call | tf_op jit(solution)/shard_map/fused/pallas_call | solution.py:335
  57.2 2.3 %copy.9 = bf16[64,8192]{1,0:T(8,128)(2,1)} copy(bf16[64,8192]{1,0:T(8,128)(2,1)} %fused.1) | data formatting | bytes 2097152

commit v4 on v3

--- a/solution.py
+++ b/solution.py
@@ -10,7 +10,7 @@
 F32, BF = jnp.float32, jnp.bfloat16
 C = 128
 NCH = 4
-HP = 2
+HP = 4
 NT = ((1,), (1,))
 TN = ((0,), (0,))
 
@@ -24,9 +24,8 @@
     return high, (x - high.astype(F32)).astype(BF)
 
 
-def dot2(a, b, dims=((1,), (0,))):
-    high, low = split(a)
-    return dotf(high, b, dims) + dotf(low, b, dims)
+def dot2(a, b):
+    return dotf(jnp.concatenate(split(a), 1), jnp.concatenate([b, b], 0))
 
 
 def inverses(lowers, ii, jj):
@@ -145,8 +144,7 @@
                 rows_c = mixed[:, 128:]
             near[n].append(near_c)
             rows[n].append(rows_c.astype(BF))
-            high, low = split(tail * errors)
-            grown = dotf(kns[i], high, TN) + dotf(kns[i], low, TN)
+            grown = dotf(jnp.concatenate([kns[i], kns[i]], 0), jnp.concatenate(split(tail * errors), 0), TN)
             if c == 0:
                 pair[n] = jnp.concatenate([jnp.zeros((128, 128), F32), fall * eye], axis=1) + grown
             else:
@@ -170,7 +168,8 @@
     pos = lax.axis_index("ctx")
     me = lax.axis_index("head")
     bits = [(pos // 2**r) % 2 for r in range(LEV)]
-    mates = [pos + (1 - 2 * bits[r]) * 2**r for r in range(LEV)]
+    x, z = pos // 4, pos % 4
+    mates = [pos + 1 - 2 * bits[0], pos + 3 - 2 * z, pos + 4 - 8 * bits[2], pos + 12 - 8 * x]
     peers = [lax.rem(me + d, HEADS) for d in range(1, HEADS)]
 
     barrier = pltpu.get_barrier_semaphore()
@@ -283,11 +282,6 @@
             box_s[h, 0] = (dotf(right[:, 128:], left[:, :128]) + right_s).astype(BF)
         run_copy(r + 1, h).start()
 
-    def steps(r, lo, hi):
-        @pl.loop(lo, hi)
-        def _(h):
-            step(r, h)
-
     pairs = HEADS // HP
 
     @pl.loop(0, pairs)
@@ -312,11 +306,21 @@
         for n, h in enumerate(heads):
             near_ref[:, head_cols(h)] = near[n]
             rows_ref[:, head_cols(h)] = rows[n]
-        for r in range(LEV - 1):
-            steps(r, HP * jnp.maximum(p - 1 - r, 0), HP * jnp.maximum(p - r, 0))
-
-    for r, p in ((1, 2), (2, 1), (0, 3), (3, 0), (2, 2), (1, 3), (3, 1), (2, 3), (3, 2), (3, 3)):
-        steps(r, HP * p, HP * p + HP)
+
+    @pl.loop(0, HP)
+    def _(h):
+        step(0, h)
+
+    for r in range(LEV - 1):
+
+        @pl.loop(0, HP)
+        def _(h):
+            step(r, h + HP)
+            step(r + 1, h)
+
+    @pl.loop(HP, HEADS)
+    def _(h):
+        step(LEV - 1, h)
 
     @pl.loop(0, HEADS)
     def _(h):

time: 59.7 us -> 54.3 us (0.910)
  Pallas kernels: 57.2 us -> 51.9 us
    pallas_call x1, Pallas kernels: 57.2 us -> 51.9 us  [fused_call(): pl.pallas_call(fused_kernel, in_specs=[hbm, hbm, hbm, vmem, vmem, vmem, p...]
where the time goes in v4:
time: 54.3 us; the launch traced here: 54.2 us
  Pallas kernels  51.9 us (96%)
  local copies, waits for them, and re-layouts  2.26 us (4%)
    pallas_call x1, Pallas kernels, fused_call(): pl.pallas_call(fused_kernel, in_specs=[hbm, hbm, hbm, vmem, vmem, vmem, p...  51.9 us
    unnamed x1, local copies, waits for them, and re-layouts  2.26 us

profile of v4, /device:TPU:1, one launch (start us, length us, event | category | flops | bytes accessed | tf_op | source)
XLA Modules:
  0.0 54.2 jit_solution(12072201633949583096)
XLA Ops:
  0.0 51.9 %fused.1 = bf16[64,8192]{1,0:T(8,128)(2,1)} custom-call(bf16[512,1024]{1,0:T(8,128)(2,1)} %q_hbm.1, bf16[512,1024]{1,0:T(8,128)(2,1)} %k_hbm.1, bf16[512,1024]{1,0:T(8,128)(2,1)} %v_hbm.1, f32[8,512]{1,0:T(8,128)} %bitcast.4, f32[8,512]{1,0:T(8,128)} %bitcast.5, f32[40,512]{1,0:T(8,128)} %bitcast.3, s32[8]{0:T(128)} %lev_ref.1), custom_call_target="tpu_custom_call" | custom-call | tf_op jit(solution)/shard_map/fused/pallas_call | solution.py:339
  51.9 2.3 %copy.9 = bf16[64,8192]{1,0:T(8,128)(2,1)} copy(bf16[64,8192]{1,0:T(8,128)(2,1)} %fused.1) | data formatting | bytes 2097152

commit v5 on v4

--- a/solution.py
+++ b/solution.py
@@ -86,7 +86,7 @@
     b_ref[...] = rate_t.T
 
 
-def local_heads(heads, q, k, v, g_all, b_all, gt_ref, bt_ref):
+def local_heads(heads, q, k, v, g_all, b_all, gt_ref, bt_ref, between):
     ii = lax.broadcasted_iota(jnp.int32, (C, C), 0)
     jj = lax.broadcasted_iota(jnp.int32, (C, C), 1)
     tri = ii >= jj
@@ -116,6 +116,7 @@
     lowers = [jnp.where(strict, bc * d * g, 0.0) for bc, d, g in zip(bcs, falls, gram)]
     scores = [(a * d).astype(BF) for a, d in zip(qk, falls)]
     inv = inverses(lowers, ii, jj)
+    between()
     egr = [jnp.exp(g) for g in grs]
     egc = [jnp.exp(g) for g in gcs]
     wv = [dot2(x * b, vv) for x, b, vv in zip(inv, brs, vs)]
@@ -157,6 +158,7 @@
 MESH = pl.DeviceIdType.MESH
 HEADS = 8
 LEV = 4
+EARLY = 3
 
 
 def fused_kernel(
@@ -293,11 +295,16 @@
         def cut(ref):
             return [ref[:, head_cols(h)] for h in heads]
 
-        near, rows, pair = local_heads(heads, cut(q_ref), cut(k_ref), cut(v_ref), g_ref[...], b_ref[...], gt_ref, bt_ref)
-
-        @pl.when(p == 0)
-        def _():
-            pl.semaphore_wait(barrier, LEV + HEADS - 1)
+        def between():
+            @pl.when(p == 0)
+            def _():
+                pl.semaphore_wait(barrier, LEV + HEADS - 1)
+
+            @pl.loop(0, EARLY * p)
+            def _(h):
+                step(0, h)
+
+        near, rows, pair = local_heads(heads, cut(q_ref), cut(k_ref), cut(v_ref), g_ref[...], b_ref[...], gt_ref, bt_ref, between)
 
         for n, h in enumerate(heads):
             run_f[h] = pair[n][:, :128]
@@ -307,16 +314,24 @@
             near_ref[:, head_cols(h)] = near[n]
             rows_ref[:, head_cols(h)] = rows[n]
 
+    @pl.loop(EARLY, HP)
+    def _(h):
+        step(0, h)
+
     @pl.loop(0, HP)
     def _(h):
-        step(0, h)
-
-    for r in range(LEV - 1):
+        step(1, h)
+
+    for r in range(2):
 
         @pl.loop(0, HP)
         def _(h):
             step(r, h + HP)
-            step(r + 1, h)
+            step(r + 2, h)
+
+    @pl.loop(HP, HEADS)
+    def _(h):
+        step(LEV - 2, h)
 
     @pl.loop(HP, HEADS)
     def _(h):

time: 54.3 us -> 50.9 us (0.937)
  Pallas kernels: 51.9 us -> 48.4 us
    pallas_call x1, Pallas kernels: 51.9 us -> 48.4 us  [fused_call(): pl.pallas_call(fused_kernel, in_specs=[hbm, hbm, hbm, vmem, vmem, vmem, p...]
where the time goes in v5:
time: 50.9 us; the launch traced here: 50.7 us
  Pallas kernels  48.4 us (95%)
  local copies, waits for them, and re-layouts  2.26 us (4%)
    pallas_call x1, Pallas kernels, fused_call(): pl.pallas_call(fused_kernel, in_specs=[hbm, hbm, hbm, vmem, vmem, vmem, p...  48.4 us
    unnamed x1, local copies, waits for them, and re-layouts  2.26 us

profile of v5, /device:TPU:1, one launch (start us, length us, event | category | flops | bytes accessed | tf_op | source)
XLA Modules:
  0.0 50.7 jit_solution(18161981737058270416)
XLA Ops:
  0.0 48.4 %fused.1 = bf16[64,8192]{1,0:T(8,128)(2,1)} custom-call(bf16[512,1024]{1,0:T(8,128)(2,1)} %q_hbm.1, bf16[512,1024]{1,0:T(8,128)(2,1)} %k_hbm.1, bf16[512,1024]{1,0:T(8,128)(2,1)} %v_hbm.1, f32[8,512]{1,0:T(8,128)} %bitcast.4, f32[8,512]{1,0:T(8,128)} %bitcast.5, f32[40,512]{1,0:T(8,128)} %bitcast.3, s32[8]{0:T(128)} %lev_ref.1), custom_call_target="tpu_custom_call" | custom-call | tf_op jit(solution)/shard_map/fused/pallas_call | solution.py:354
  48.4 2.3 %copy.9 = bf16[64,8192]{1,0:T(8,128)(2,1)} copy(bf16[64,8192]{1,0:T(8,128)(2,1)} %fused.1) | data formatting | bytes 2097152

commit v6 on v4

--- a/solution.py
+++ b/solution.py
@@ -10,7 +10,6 @@
 F32, BF = jnp.float32, jnp.bfloat16
 C = 128
 NCH = 4
-HP = 4
 NT = ((1,), (1,))
 TN = ((0,), (0,))
 
@@ -86,7 +85,7 @@
     b_ref[...] = rate_t.T
 
 
-def local_heads(heads, q, k, v, g_all, b_all, gt_ref, bt_ref):
+def local_heads(heads, q, k, v, g_all, b_all, gt_ref, bt_ref, between):
     ii = lax.broadcasted_iota(jnp.int32, (C, C), 0)
     jj = lax.broadcasted_iota(jnp.int32, (C, C), 1)
     tri = ii >= jj
@@ -116,6 +115,7 @@
     lowers = [jnp.where(strict, bc * d * g, 0.0) for bc, d, g in zip(bcs, falls, gram)]
     scores = [(a * d).astype(BF) for a, d in zip(qk, falls)]
     inv = inverses(lowers, ii, jj)
+    between()
     egr = [jnp.exp(g) for g in grs]
     egc = [jnp.exp(g) for g in gcs]
     wv = [dot2(x * b, vv) for x, b, vv in zip(inv, brs, vs)]
@@ -157,6 +157,7 @@
 MESH = pl.DeviceIdType.MESH
 HEADS = 8
 LEV = 4
+GROUPS = ((0, 2), (2, 6), (6, 8))
 
 
 def fused_kernel(
@@ -179,13 +180,14 @@
         pl.semaphore_signal(barrier, inc=1, device_id={"head": j}, device_id_type=MESH)
 
     def in_copies(p):
-        cols = pl.ds(pl.multiple_of(p * HP * 128, HP * 128), HP * 128)
+        lo, hi = GROUPS[p]
+        cols = pl.ds(lo * 128, (hi - lo) * 128)
         return [
             pltpu.make_async_copy(src.at[:, cols], dst.at[:, cols], in_sem.at[i, p])
             for i, (src, dst) in enumerate(((k_hbm, k_ref), (q_hbm, q_ref), (v_hbm, v_ref)))
         ]
 
-    for p in range(HEADS // HP):
+    for p in range(len(GROUPS)):
         for c in in_copies(p):
             c.start()
 
@@ -204,6 +206,8 @@
         )
 
     def head_cols(h):
+        if isinstance(h, int):
+            return pl.ds(h * 128, 128)
         return pl.ds(pl.multiple_of(h * 128, 128), 128)
 
     def out_copy(h, src_dev, dst_dev):
@@ -282,23 +286,26 @@
             box_s[h, 0] = (dotf(right[:, 128:], left[:, :128]) + right_s).astype(BF)
         run_copy(r + 1, h).start()
 
-    pairs = HEADS // HP
-
-    @pl.loop(0, pairs)
-    def _(p):
+    def steps(todo):
+        for r, lo, hi in todo:
+
+            @pl.loop(lo, hi)
+            def _(h):
+                step(r, h)
+
+    def local_group(p, inside):
         for c in in_copies(p):
             c.wait()
-        heads = [p * HP + n for n in range(HP)]
+        heads = list(range(*GROUPS[p]))
 
         def cut(ref):
             return [ref[:, head_cols(h)] for h in heads]
 
-        near, rows, pair = local_heads(heads, cut(q_ref), cut(k_ref), cut(v_ref), g_ref[...], b_ref[...], gt_ref, bt_ref)
-
-        @pl.when(p == 0)
-        def _():
+        near, rows, pair = local_heads(
+            heads, cut(q_ref), cut(k_ref), cut(v_ref), g_ref[...], b_ref[...], gt_ref, bt_ref, lambda: steps(inside)
+        )
+        if p == 0:
             pl.semaphore_wait(barrier, LEV + HEADS - 1)
-
         for n, h in enumerate(heads):
             run_f[h] = pair[n][:, :128]
             box[0, h, 0] = pair[n].astype(BF)
@@ -307,20 +314,12 @@
             near_ref[:, head_cols(h)] = near[n]
             rows_ref[:, head_cols(h)] = rows[n]
 
-    @pl.loop(0, HP)
-    def _(h):
-        step(0, h)
-
-    for r in range(LEV - 1):
-
-        @pl.loop(0, HP)
-        def _(h):
-            step(r, h + HP)
-            step(r + 1, h)
-
-    @pl.loop(HP, HEADS)
-    def _(h):
-        step(LEV - 1, h)
+    local_group(0, ())
+    local_group(1, ((0, 0, 2),))
+    steps(((1, 0, 2),))
+    local_group(2, ((0, 2, 4), (2, 0, 2)))
+    steps(((0, 4, 6), (1, 2, 4), (3, 0, 2), (0, 6, 8), (1, 4, 6), (2, 2, 4), (1, 6, 8), (2, 4, 6), (3, 2, 4)))
+    steps(((2, 6, 8), (3, 4, 6), (3, 6, 8)))
 
     @pl.loop(0, HEADS)
     def _(h):
@@ -357,7 +356,7 @@
             pltpu.VMEM((HEADS, 128, LEV * 128), BF),
             pltpu.VMEM((512, 40), F32),
             pltpu.VMEM((512, 1024), BF),
-            pltpu.SemaphoreType.DMA((3, HEADS // HP)),
+            pltpu.SemaphoreType.DMA((3, len(GROUPS))),
             pltpu.SemaphoreType.DMA((LEV, HEADS)),
             pltpu.SemaphoreType.DMA((LEV, HEADS)),
             pltpu.SemaphoreType.DMA((HEADS, HEADS)),

time: 54.3 us -> 51.6 us (0.950)
  Pallas kernels: 51.9 us -> 49.1 us
    pallas_call x1, Pallas kernels: 51.9 us -> 49.1 us  [fused_call(): pl.pallas_call(fused_kernel, in_specs=[hbm, hbm, hbm, vmem, vmem, vmem, p...]
where the time goes in v6:
time: 51.6 us; the launch traced here: 51.4 us
  Pallas kernels  49.1 us (95%)
  local copies, waits for them, and re-layouts  2.26 us (4%)
    pallas_call x1, Pallas kernels, fused_call(): pl.pallas_call(fused_kernel, in_specs=[hbm, hbm, hbm, vmem, vmem, vmem, p...  49.1 us
    unnamed x1, local copies, waits for them, and re-layouts  2.26 us

profile of v6, /device:TPU:1, one launch (start us, length us, event | category | flops | bytes accessed | tf_op | source)
XLA Modules:
  0.0 51.4 jit_solution(6127878179243973377)
XLA Ops:
  0.0 49.1 %fused.1 = bf16[64,8192]{1,0:T(8,128)(2,1)} custom-call(bf16[512,1024]{1,0:T(8,128)(2,1)} %q_hbm.1, bf16[512,1024]{1,0:T(8,128)(2,1)} %k_hbm.1, bf16[512,1024]{1,0:T(8,128)(2,1)} %v_hbm.1, f32[8,512]{1,0:T(8,128)} %bitcast.4, f32[8,512]{1,0:T(8,128)} %bitcast.5, f32[40,512]{1,0:T(8,128)} %bitcast.3, s32[8]{0:T(128)} %lev_ref.1), custom_call_target="tpu_custom_call" | custom-call | tf_op jit(solution)/shard_map/fused/pallas_call | solution.py:338
  49.2 2.3 %copy.9 = bf16[64,8192]{1,0:T(8,128)(2,1)} copy(bf16[64,8192]{1,0:T(8,128)(2,1)} %fused.1) | data formatting | bytes 2097152
